TPU v7x, 256 devices: a whole 4x4x8 slice. The times are simulated.
256 devices in a mesh: chan: 16 (over y_hi, z), strip: 16 (over y_lo, x, core).
Axes of the slice: x: 4, y: 4 (y_hi: 2, y_lo: 2; y = y_hi * 2 + y_lo), z: 8, core: 2. Of those that a mesh axis runs over, the one named last changes fastest.
Arguments:
- image: bfloat16 [256, 48, 1280], P('chan', 'strip'), may hold values from -6 to 6
- filter_one: bfloat16 [256, 9, 256], P('strip', None, 'chan'), may hold values from -0.125 to 0.125
- filter_two: bfloat16 [256, 9, 256], P('strip', None, 'chan'), may hold values from -0.125 to 0.125
- cotangent: bfloat16 [256, 48, 1280], P('chan', 'strip'), may hold values from -6 to 6
Outputs:
- image_grad: bfloat16 [256, 48, 1280], P('chan', 'strip')
- grad_one: float32 [256, 9, 256], P('strip', None, 'chan')
- grad_two: float32 [256, 9, 256], P('strip', None, 'chan')
All inputs are finite; a program needn't handle non-finite values.
Results may differ from a plain program's by a relative error of at most 0.018.
Values may be sent and summed in bfloat16 or wider, within the bound.
No kernel may reach another device: no remote copies, remote signals or barrier semaphores. Data moves between devices by JAX's collectives and lax.ppermute only.
A program may use at most 64 MiB of HBM per device.

v0:
```python
import functools
import math

import jax
import jax.numpy as jnp
from jax import lax
from jax.experimental import pallas as pl
from jax.experimental.pallas import tpu as pltpu
from jax.sharding import Mesh
from jax.sharding import PartitionSpec as P

AXES = ("yh", "z", "yl", "x", "core")
CHAN = ("yh", "z")
STRIP = ("yl", "x", "core")
TORUS = ("yh", "yl", "x")
F32 = jnp.float32
BF16 = jnp.bfloat16

W = 32


def call(kernel, outs, scratch, args, prefetch, room=10):
    return pl.pallas_call(
        kernel,
        out_shape=outs,
        in_specs=[pl.BlockSpec(memory_space=pltpu.SMEM)]
        + [pl.BlockSpec(memory_space=pltpu.VMEM)] * len(args),
        out_specs=jax.tree.map(lambda _: pl.BlockSpec(memory_space=pltpu.VMEM), outs),
        scratch_shapes=scratch,
        compiler_params=pltpu.CompilerParams(vmem_limit_bytes=room * 2**20),
    )(prefetch, *args)


def shape(dims, kind=BF16):
    return jax.ShapeDtypeStruct(dims, kind)


def windows_kernel(at, image, cotangent, pieces, *rest):
    windows, image_wide, cotangent_wide = rest
    for wide, source in ((image_wide, image), (cotangent_wide, cotangent)):
        wide[:, :256] = jnp.zeros((48, 256), F32)
        wide[:, 1536:] = jnp.zeros((48, 256), F32)
        wide[:, 256:1536] = source[...].astype(F32)
    lane = lax.broadcasted_iota(jnp.int32, (48, 384), 1)
    for z in range(8):
        first = 256 + 160 * z - 8
        base = first // 128 * 128
        left = pltpu.roll(image_wide[:, base : base + 384], 384 - (first - base), 1)
        second = 256 + 160 * z - 4 - 176
        base = second // 128 * 128
        right = pltpu.roll(cotangent_wide[:, base : base + 512], 512 - (second - base), 1)[:, :384]
        windows[z, :48, :] = jnp.where(lane < 176, left, right).astype(BF16)
        windows[z, 48:, :] = pieces[...]


def turn_kernel(at, *rest):
    held, outs, turned, chunk = rest
    for i in range(3):
        turned[...] = held[:, 16 * i : 16 * i + 16, :].reshape(128, 384).astype(F32).T
        for j in range(16):
            chunk[:32, :] = turned[10 * j : 10 * j + 32, :]
            chunk[26:48, :] = turned[176 + 10 * j : 198 + 10 * j, :]
            outs[j, 48 * i : 48 * i + 48, :] = chunk[...].astype(BF16)
    filters = held[:, 48:, :].reshape(128, 384).astype(F32).T[:288].astype(BF16)
    for j in range(16):
        outs[j, 144:, :] = filters


def sigmoid(v):
    return 1.0 / (1.0 + jnp.exp(-v))


def conv_kernel(at, *rest):
    own, other = rest[:2]
    send, keep, image_send, image_keep = rest[2:6]
    acts, wide, pre, hidden, second, first, mine, terms, image_rows = rest[6:]
    y, x, core, z = at[2], at[3], at[4], at[1]
    acts[:8] = jnp.zeros((8, 48, 256), BF16)
    acts[56:] = jnp.zeros((8, 48, 256), BF16)
    for pieces, side in ((own, core), (other, 1 - core)):
        for j in range(16):
            half = j // 8
            strip = 2 * (j % 8) + side
            lanes = slice(half * 128, half * 128 + 128)
            acts[pl.ds(3 * strip + 8, 3), :, lanes] = pieces[j, :144, :].reshape(3, 48, 128)
            wide[:, strip, :, lanes] = pieces[j, 144:, :].reshape(18, 16, 128)

    top = 24 * core - 8
    left = 160 * z + 10 * (4 * y + x) - 8

    def inside(start, rows):
        r = lax.broadcasted_iota(jnp.int32, (rows, W, 256), 0) + (top + start)
        c = lax.broadcasted_iota(jnp.int32, (rows, W, 256), 1) + left
        return (r >= 0) & (r < 48) & (c >= 0) & (c < 1280)

    def tap(which, i, j):
        return wide[9 * which + 3 * i + j].reshape(256, 256)

    def ahead(source, start, rows, which):
        band = jnp.concatenate(
            [source[pl.ds(start + 2 * i - 2, rows), :W, :] for i in range(3)], axis=-1
        ).reshape(rows * W, 768)
        total = None
        for j in range(3):
            weights = jnp.concatenate([tap(which, i, j) for i in range(3)], axis=0)
            term = jnp.dot(band, weights, preferred_element_type=F32)
            if j != 1:
                term = pltpu.roll(term, (rows * W - 2 * (j - 1)) % (rows * W), 0)
            total = term if total is None else total + term
        return total.reshape(rows, W, 256)

    def backward(source, start, rows, which):
        band = jnp.concatenate(
            [source[pl.ds(start - 2 * i + 2, rows), :, :] for i in range(3)], axis=-1
        ).reshape(rows * W, 768)
        total = None
        for j in range(3):
            weights = jnp.concatenate([tap(which, i, j) for i in range(3)], axis=1)
            term = lax.dot_general(
                band, weights, (((1,), (1,)), ((), ())), preferred_element_type=F32
            )
            if j != 1:
                term = pltpu.roll(term, (rows * W + 2 * (j - 1)) % (rows * W), 0)
            total = term if total is None else total + term
        return total.reshape(rows, W, 256)

    def slope(v):
        s = sigmoid(v)
        return s * (1.0 + v * (1.0 - s))

    def each(start, count, rows, body):
        def step(k, _):
            body(start + k * rows)
            return 0

        lax.fori_loop(0, count, step, 0)

    def first_step(start):
        rows = 12
        value = ahead(acts, start + 24 * core, rows, 0)
        pre[pl.ds(start, rows)] = value
        value = jnp.where(inside(start, rows), value * sigmoid(value), 0.0)
        hidden[pl.ds(start, rows)] = value.astype(BF16)

    each(2, 3, 12, first_step)

    def second_step(start):
        rows = 16
        value = ahead(hidden, start, rows, 1)
        got = acts[pl.ds(start + 24 * core, rows), 16:, :].astype(F32).reshape(rows * W, 256)
        got = pltpu.roll(got, rows * W - 6, 0).reshape(rows, W, 256)
        value = jnp.where(inside(start, rows), got * slope(value), 0.0)
        second[pl.ds(start, rows)] = value.astype(BF16)

    each(4, 2, 16, second_step)

    def third_step(start):
        rows = 14
        value = backward(second, start, rows, 1)
        value = jnp.where(inside(start, rows), value * slope(pre[pl.ds(start, rows)]), 0.0)
        first[pl.ds(start, rows)] = value.astype(BF16)

    each(6, 2, 14, third_step)

    def fourth_step(start):
        rows = 12
        value = backward(first, start, rows, 0)
        image_rows[pl.ds(start - 8, rows)] = value[:, 8:24, :].astype(BF16)

    each(8, 2, 12, fourth_step)
    for side, out in ((1 - core, image_send), (core, image_keep)):
        for k in range(4):
            for half in range(2):
                out[half, k] = image_rows[
                    pl.ds(6 * k + 3 * side, 3), :, 128 * half : 128 * half + 128
                ].reshape(48, 128)

    def weight_terms(values, grads, which):
        turned = values.reshape(28 * W, 256).astype(F32).T.astype(BF16)
        column = lax.broadcasted_iota(jnp.int32, (24, W, 256), 1)
        chosen = jnp.where((column >= 8) & (column < 18), grads[8:32].astype(F32), 0.0)
        chosen = chosen.reshape(24 * W, 256)
        for j in range(3):
            shifted = chosen
            if j != 1:
                shifted = pltpu.roll(chosen, (24 * W + 2 * (j - 1)) % (24 * W), 0)
            mine[j, 8:32] = shifted.reshape(24, W, 256).astype(BF16)
        def step(i, _):
            for j in range(3):
                rows = mine[j, pl.ds(8 - 2 * i, 28)].reshape(28 * W, 256)
                got = jnp.dot(turned, rows, preferred_element_type=F32).astype(BF16)
                got = got.reshape(8, 2, 16, 256)
                for side in range(2):
                    for half in range(2):
                        terms[side, half, :, 9 * which + 3 * i + j] = got[
                            :, side, :, 128 * half : 128 * half + 128
                        ]
            return 0

        lax.fori_loop(0, 3, step, 0)

    for j in range(3):
        mine[j, :8] = jnp.zeros((8, W, 256), BF16)
        mine[j, 32:] = jnp.zeros((8, W, 256), BF16)
    weight_terms(hidden[6:34], second, 1)
    weight_terms(acts[pl.ds(6 + 24 * core, 28), :W, :], first, 0)
    send[...] = terms[1 - core].reshape(2, 8, 288, 128)
    keep[...] = terms[core].reshape(2, 8, 288, 128)


def scatter_kernel(at, keep, got, image_keep, image_got, outs):
    for j in range(16):
        half, q = j // 8, j % 8
        outs[j, :288, :] = (keep[half, q].astype(F32) + got[half, q].astype(F32)).astype(BF16)
    for half in range(2):
        for k in range(4):
            outs[8 * half + 4 * at[4] + k, 288:, :] = image_keep[half, k]
            outs[8 * half + 4 - 4 * at[4] + k, 288:, :] = image_got[half, k]


def regroup_kernel(at, *rest):
    pieces, windows, columns = rest
    total = None
    for j in range(16):
        term = pieces[j, :288, :].astype(F32)
        total = term if total is None else total + term
    total = jnp.concatenate([total, jnp.zeros((96, 128), F32)], axis=0).T.astype(BF16)
    for z in range(8):
        windows[z, 48:, :] = total[16 * z : 16 * z + 16]
        windows[z, :48, 256:] = jnp.zeros((48, 128), BF16)
    columns[...] = jnp.zeros((256, 128), F32)
    for i in range(3):
        for j in range(16):
            columns[10 * j : 10 * j + 16, :] = pieces[j, 288 + 16 * i : 304 + 16 * i, :].astype(
                F32
            )
        turned = columns[...].T.astype(BF16)
        for z in range(8):
            windows[z, 16 * i : 16 * i + 16, :256] = turned[16 * z : 16 * z + 16]


def finish_kernel(scale, at, *rest):
    pieces, image_out, filters_out, wide = rest
    total = None
    for z in range(8):
        term = pieces[z, 48:, :].astype(F32)
        total = term if total is None else total + term
    filters_out[...] = total * scale
    lane = lax.broadcasted_iota(jnp.int32, (48, 384), 1)
    wide[...] = jnp.zeros((48, 1536), F32)
    for z in range(8):
        base = 160 * z // 128 * 128
        off = 160 * z - base
        value = pieces[z, :48, :].astype(F32)
        if off:
            value = pltpu.roll(value, off, 1)
        wide[:, base : base + 384] = jnp.where(
            (lane >= off) & (lane < off + 160), value, wide[:, base : base + 384]
        )
    image_out[...] = wide[:, :1280].astype(BF16)


def exchanged(array, axes):
    return lax.all_to_all(array, axes, split_axis=0, concat_axis=0, tiled=True)


def swapped(array):
    return lax.ppermute(array, "core", [(0, 1), (1, 0)])


def local(image, filter_one, filter_two, cotangent):
    scale = 1.0 / math.sqrt(48 * 1280)
    yh, z, yl, x, core = (lax.axis_index(a) for a in AXES)
    at = jnp.stack([yh, z, 2 * yh + yl, x, core]).astype(jnp.int32)

    def rows_first(a):
        return jnp.transpose(a, (1, 0, 2)).reshape(48, 1280)

    filters = jnp.concatenate(
        [jnp.transpose(f, (2, 1, 0)).reshape(16, 144) for f in (filter_one, filter_two)]
        + [jnp.zeros((16, 96), BF16)],
        axis=1,
    )
    pieces = call(
        windows_kernel,
        shape((8, 64, 384)),
        [pltpu.VMEM((48, 1792), F32), pltpu.VMEM((48, 1792), F32)],
        [rows_first(image), rows_first(cotangent), filters],
        at,
    )
    pieces = call(
        turn_kernel,
        shape((16, 432, 128)),
        [pltpu.VMEM((384, 128), F32), pltpu.VMEM((48, 128), F32)],
        [exchanged(pieces, "z")],
        at,
    )
    pieces = exchanged(pieces, TORUS)
    send, keep, image_send, image_keep = call(
        conv_kernel,
        [shape((2, 8, 288, 128))] * 2 + [shape((2, 4, 48, 128))] * 2,
        [
            pltpu.VMEM((64, 48, 256), BF16),
            pltpu.VMEM((18, 16, 16, 256), BF16),
            pltpu.VMEM((40, W, 256), F32),
            pltpu.VMEM((40, W, 256), BF16),
            pltpu.VMEM((40, W, 256), BF16),
            pltpu.VMEM((40, W, 256), BF16),
            pltpu.VMEM((3, 40, W, 256), BF16),
            pltpu.VMEM((2, 2, 8, 18, 16, 128), BF16),
            pltpu.VMEM((24, 16, 256), BF16),
        ],
        [pieces, swapped(pieces)],
        at,
        28,
    )
    pieces = call(
        scatter_kernel,
        shape((16, 336, 128)),
        [],
        [keep, swapped(send), image_keep, swapped(image_send)],
        at,
    )
    pieces = call(
        regroup_kernel,
        shape((8, 64, 384)),
        [pltpu.VMEM((256, 128), F32)],
        [exchanged(pieces, TORUS)],
        at,
    )
    image_grad, filter_grads = call(
        functools.partial(finish_kernel, scale),
        [shape((48, 1280)), shape((16, 384), F32)],
        [pltpu.VMEM((48, 1536), F32)],
        [exchanged(pieces, "z")],
        at,
    )
    grad_one, grad_two = (
        jnp.transpose(filter_grads[:, 144 * k : 144 * k + 144].reshape(16, 9, 16), (2, 1, 0))
        for k in range(2)
    )
    return jnp.transpose(image_grad.reshape(3, 16, 1280), (1, 0, 2)), grad_one, grad_two


def solution(mesh):
    finer = Mesh(mesh.devices.reshape(2, 8, 2, 4, 2), AXES)
    return jax.shard_map(
        local,
        mesh=finer,
        in_specs=(
            P(CHAN, STRIP, None),
            P(STRIP, None, CHAN),
            P(STRIP, None, CHAN),
            P(CHAN, STRIP, None),
        ),
        out_specs=(P(CHAN, STRIP, None), P(STRIP, None, CHAN), P(STRIP, None, CHAN)),
        check_vma=False,
    )
```

profile of v0, /device:TPU:8, one launch (start us, length us, event | category | flops | bytes accessed | tf_op | source)
XLA Modules:
  0.0 123.0 jit_solution(3772516136177484843)
XLA Ops:
  0.6 0.8 copy.11
  1.5 0.8 copy.12
  2.3 0.1 pad.2.clone
  2.4 0.1 maximum_maximum_fusion.pieces
  2.5 0.1 stack.23.at
  2.6 0.9 copy-done
  3.5 0.9 copy-done.1
  4.4 0.8 shard_map.67
  5.1 22.9 %all_to_all.20.rest_0_ = bf16[8,64,384]{2,1,0:T(8,128)(2,1)S(1)} all-to-all(bf16[8,64,384]{2,1,0:T(8,128)(2,1)S(1)} %shard_map.67), channel_id=1, replica_groups=mesh['yh'=2,'z'=8,'yl'=2,'x'=4,'core'=2] {'z'}, dimensions={0} | all-to-all | bytes 786432 | tf_op jit(solution)/shard_map/all_to_all | solution.py:264
  28.1 1.0 shard_map.68
  29.1 29.5 %all_to_all.21.rest_0_ = bf16[16,432,128]{2,1,0:T(8,128)(2,1)S(1)} all-to-all(bf16[16,432,128]{2,1,0:T(8,128)(2,1)S(1)} %shard_map.68), channel_id=1, replica_groups=mesh['yh'=2,'z'=8,'yl'=2,'x'=4,'core'=2] {'yh','yl','x'}, dimensions={0} | all-to-all | bytes 3538944 | tf_op jit(solution)/shard_map/all_to_all | solution.py:264
  58.5 3.7 %collective-permute-done.rest_1_ = bf16[16,432,128]{2,1,0:T(8,128)(2,1)S(1)} collective-permute-done((bf16[16,432,128]{2,1,0:T(8,128)(2,1)S(1)}, bf16[16,432,128]{2,1,0:T(8,128)(2,1)S(1)}, u32[]{:S(2)}, u32[]{:S(2)}) %collective-permute-start) | collective-permute-done | bytes 1769504 | tf_op jit(solution)/shard_map/ppermute | solution.py:268
  62.2 12.8 %shard_map.69 = (bf16[2,8,288,128]{3,2,1,0:T(8,128)(2,1)S(1)}, bf16[2,8,288,128]{3,2,1,0:T(8,128)(2,1)S(1)}, bf16[2,4,48,128]{3,2,1,0:T(8,128)(2,1)S(1)}, bf16[2,4,48,128]{3,2,1,0:T(8,128)(2,1)S(1)}) custom-call(s32[5]{0:T(128)S(1)} %stack.23.at, bf16[16,432,128]{2,1,0:T(8,128)(2,1)S(1)} %all_to_all.21.rest_0_, ...), custom_call_target="tpu_custom_call" | custom-call | tf_op jit(solution)/shard_map/pallas_call | solution.py:23
  75.0 0.2 collective-permute-start.1
  75.3 0.4 collective-permute-start.2
  75.6 2.5 %collective-permute-done.2.image_got = bf16[2,4,48,128]{3,2,1,0:T(8,128)(2,1)S(1)} collective-permute-done((bf16[2,4,48,128]{3,2,1,0:T(8,128)(2,1)S(1)}, bf16[2,4,48,128]{3,2,1,0:T(8,128)(2,1)S(1)}, u32[]{:S(2)}, u32[]{:S(2)}) %collective-permute-start.2) | collective-permute-done | bytes 98336 | tf_op jit(solution)/shard_map/ppermute | solution.py:268
  78.1 0.8 shard_map.70
  78.9 24.1 %all_to_all.22.rest_0_ = bf16[16,336,128]{2,1,0:T(8,128)(2,1)S(1)} all-to-all(bf16[16,336,128]{2,1,0:T(8,128)(2,1)S(1)} %shard_map.70), channel_id=1, replica_groups=mesh['yh'=2,'z'=8,'yl'=2,'x'=4,'core'=2] {'yh','yl','x'}, dimensions={0} | all-to-all | bytes 2752512 | tf_op jit(solution)/shard_map/all_to_all | solution.py:264
  103.0 0.8 shard_map.71
  103.9 16.2 %all_to_all.23.rest_0_ = bf16[8,64,384]{2,1,0:T(8,128)(2,1)S(1)} all-to-all(bf16[8,64,384]{2,1,0:T(8,128)(2,1)S(1)} %shard_map.71), channel_id=1, replica_groups=mesh['yh'=2,'z'=8,'yl'=2,'x'=4,'core'=2] {'z'}, dimensions={0} | all-to-all | bytes 786432 | tf_op jit(solution)/shard_map/all_to_all | solution.py:264
  120.1 1.3 %shard_map.72 = (bf16[48,1280]{1,0:T(8,128)(2,1)}, f32[16,384]{1,0:T(8,128)S(1)}) custom-call(s32[5]{0:T(128)S(1)} %stack.23.at, bf16[8,64,384]{2,1,0:T(8,128)(2,1)S(1)} %all_to_all.23.rest_0_), custom_call_target="tpu_custom_call" | custom-call | tf_op jit(solution)/shard_map/pallas_call | solution.py:23
  121.4 0.1 fusion
  121.5 0.7 copy.14
  122.2 0.7 copy.13
  (5 shorter events, 0.0 us)
Async XLA Ops:
  2.6 0.9 copy-start
  3.5 0.9 copy-start.1
  58.5 3.7 %collective-permute-start = (bf16[16,432,128]{2,1,0:T(8,128)(2,1)S(1)}, bf16[16,432,128]{2,1,0:T(8,128)(2,1)S(1)}, u32[]{:S(2)}, u32[]{:S(2)}) collective-permute-start(bf16[16,432,128]{2,1,0:T(8,128)(2,1)S(1)} %all_to_all.21.rest_0_), channel_id=1, source_target_pairs={{0,1},{1,0},{2,3},{3,2},{4,5},{5,4},{6,7},{7,6},{8,9},{9,8},{10,11... | collective-permute-start | bytes 5308424 | tf_op jit(solution)/shard_map/ppermute | solution.py:268
  75.0 3.1 %collective-permute-start.1 = (bf16[2,8,288,128]{3,2,1,0:T(8,128)(2,1)S(1)}, bf16[2,8,288,128]{3,2,1,0:T(8,128)(2,1)S(1)}, u32[]{:S(2)}, u32[]{:S(2)}) collective-permute-start(bf16[2,8,288,128]{3,2,1,0:T(8,128)(2,1)S(1)} %get-tuple-element.10), channel_id=1, source_target_pairs={{0,1},{1,0},{2,3},{3,2},{4,5},{5,4},{6,7},{7,6},{8,9},{9,8},{10,11... | collective-permute-start | bytes 3538952 | tf_op jit(solution)/shard_map/ppermute | solution.py:268
  75.3 2.8 %collective-permute-start.2 = (bf16[2,4,48,128]{3,2,1,0:T(8,128)(2,1)S(1)}, bf16[2,4,48,128]{3,2,1,0:T(8,128)(2,1)S(1)}, u32[]{:S(2)}, u32[]{:S(2)}) collective-permute-start(bf16[2,4,48,128]{3,2,1,0:T(8,128)(2,1)S(1)} %get-tuple-element.12), channel_id=1, source_target_pairs={{0,1},{1,0},{2,3},{3,2},{4,5},{5,4},{6,7},{7,6},{8,9},{9,8},{10,11... | collective-permute-start | bytes 294920 | tf_op jit(solution)/shard_map/ppermute | solution.py:268
where the time goes:
time: 125 us; the launch traced here: 123 us
  blocking collectives  92.7 us (74%)
  Pallas kernels  17.5 us (14%)
  waiting for transfers between devices  6.17 us (5%)
  local copies, waits for them, and re-layouts  5.19 us (4%)
    all_to_all x4, blocking collectives, exchanged(): return lax.all_to_all(array, axes, split_axis=0, concat_axis=0, tiled=True)  92.7 us
    pallas_call x6, Pallas kernels, call(): pl.pallas_call(kernel, out_shape=outs, in_specs=[pl.BlockSpec(memory_spac...  17.5 us
    ppermute x3, waiting for transfers between devices, swapped(): return lax.ppermute(array, 'core', [(0, 1), (1, 0)])  6.17 us
  transfers between devices with their start and end apart: 3, of which 2 were waited for; matrix products, arithmetic and copies ran while one was open for 0% of the time, Pallas kernels for 0%

commit v1 on v0

--- a/solution.py
+++ b/solution.py
@@ -19,12 +19,12 @@
 W = 32
 
 
-def call(kernel, outs, scratch, args, prefetch, room=10):
+def call(kernel, outs, scratch, args, prefetch, room=10, space=pltpu.VMEM):
     return pl.pallas_call(
         kernel,
         out_shape=outs,
         in_specs=[pl.BlockSpec(memory_space=pltpu.SMEM)]
-        + [pl.BlockSpec(memory_space=pltpu.VMEM)] * len(args),
+        + [pl.BlockSpec(memory_space=space)] * len(args),
         out_specs=jax.tree.map(lambda _: pl.BlockSpec(memory_space=pltpu.VMEM), outs),
         scratch_shapes=scratch,
         compiler_params=pltpu.CompilerParams(vmem_limit_bytes=room * 2**20),
@@ -35,8 +35,33 @@
     return jax.ShapeDtypeStruct(dims, kind)
 
 
-def windows_kernel(at, image, cotangent, pieces, *rest):
-    windows, image_wide, cotangent_wide = rest
+def windows_kernel(at, *rest):
+    sources, (windows, image_wide, cotangent_wide), held, arrived = (
+        rest[:4],
+        rest[4:7],
+        rest[7:11],
+        rest[11],
+    )
+    copies = [
+        pltpu.make_async_copy(a, b, arrived.at[k]) for k, (a, b) in enumerate(zip(sources, held))
+    ]
+    for copy in copies:
+        copy.start()
+    for copy in copies:
+        copy.wait()
+    image, cotangent, filter_one, filter_two = held
+    row = lax.broadcasted_iota(jnp.int32, (16, 16), 0)
+    unit = (row == lax.broadcasted_iota(jnp.int32, (16, 16), 1)).astype(F32).astype(BF16)
+    pieces = jnp.concatenate(
+        [
+            lax.dot_general(
+                unit, f[...], (((1,), (1,)), ((), ())), preferred_element_type=F32
+            )
+            for f in (filter_one, filter_two)
+        ]
+        + [jnp.zeros((16, 96), F32)],
+        axis=1,
+    ).astype(BF16)
     for wide, source in ((image_wide, image), (cotangent_wide, cotangent)):
         wide[:, :256] = jnp.zeros((48, 256), F32)
         wide[:, 1536:] = jnp.zeros((48, 256), F32)
@@ -50,7 +75,7 @@
         base = second // 128 * 128
         right = pltpu.roll(cotangent_wide[:, base : base + 512], 512 - (second - base), 1)[:, :384]
         windows[z, :48, :] = jnp.where(lane < 176, left, right).astype(BF16)
-        windows[z, 48:, :] = pieces[...]
+        windows[z, 48:, :] = pieces
 
 
 def turn_kernel(at, *rest):
@@ -67,7 +92,7 @@
 
 
 def sigmoid(v):
-    return 1.0 / (1.0 + jnp.exp(-v))
+    return 0.5 + 0.5 * jnp.tanh(0.5 * v)
 
 
 def conv_kernel(at, *rest):
@@ -85,13 +110,25 @@
             acts[pl.ds(3 * strip + 8, 3), :, lanes] = pieces[j, :144, :].reshape(3, 48, 128)
             wide[:, strip, :, lanes] = pieces[j, 144:, :].reshape(18, 16, 128)
 
-    top = 24 * core - 8
-    left = 160 * z + 10 * (4 * y + x) - 8
-
-    def inside(start, rows):
-        r = lax.broadcasted_iota(jnp.int32, (rows, W, 256), 0) + (top + start)
-        c = lax.broadcasted_iota(jnp.int32, (rows, W, 256), 1) + left
-        return (r >= 0) & (r < 48) & (c >= 0) & (c < 1280)
+    at_left = (z == 0) & (y + x == 0)
+    at_right = (z == 7) & (y + x == 6)
+
+    def cleared(target):
+        @pl.when(core == 0)
+        def _():
+            target[:8] = jnp.zeros((8, W, 256), BF16)
+
+        @pl.when(core == 1)
+        def _():
+            target[32:] = jnp.zeros((8, W, 256), BF16)
+
+        @pl.when(at_left)
+        def _():
+            target[:, :8, :] = jnp.zeros((40, 8, 256), BF16)
+
+        @pl.when(at_right)
+        def _():
+            target[:, 18:, :] = jnp.zeros((40, 14, 256), BF16)
 
     def tap(which, i, j):
         return wide[9 * which + 3 * i + j].reshape(256, 256)
@@ -139,28 +176,28 @@
         rows = 12
         value = ahead(acts, start + 24 * core, rows, 0)
         pre[pl.ds(start, rows)] = value
-        value = jnp.where(inside(start, rows), value * sigmoid(value), 0.0)
-        hidden[pl.ds(start, rows)] = value.astype(BF16)
+        hidden[pl.ds(start, rows)] = (value * sigmoid(value)).astype(BF16)
 
     each(2, 3, 12, first_step)
+    cleared(hidden)
 
     def second_step(start):
         rows = 16
         value = ahead(hidden, start, rows, 1)
         got = acts[pl.ds(start + 24 * core, rows), 16:, :].astype(F32).reshape(rows * W, 256)
         got = pltpu.roll(got, rows * W - 6, 0).reshape(rows, W, 256)
-        value = jnp.where(inside(start, rows), got * slope(value), 0.0)
-        second[pl.ds(start, rows)] = value.astype(BF16)
+        second[pl.ds(start, rows)] = (got * slope(value)).astype(BF16)
 
     each(4, 2, 16, second_step)
+    cleared(second)
 
     def third_step(start):
         rows = 14
         value = backward(second, start, rows, 1)
-        value = jnp.where(inside(start, rows), value * slope(pre[pl.ds(start, rows)]), 0.0)
-        first[pl.ds(start, rows)] = value.astype(BF16)
+        first[pl.ds(start, rows)] = (value * slope(pre[pl.ds(start, rows)])).astype(BF16)
 
     each(6, 2, 14, third_step)
+    cleared(first)
 
     def fourth_step(start):
         rows = 12
@@ -175,19 +212,22 @@
                     pl.ds(6 * k + 3 * side, 3), :, 128 * half : 128 * half + 128
                 ].reshape(48, 128)
 
+    def narrowed(values, rows, shift):
+        flat = values.astype(F32).reshape(rows * W, 256)
+        flat = pltpu.roll(flat, (rows * W + shift) % (rows * W), 0)
+        return flat.reshape(rows, W, 256)[:, :16, :]
+
     def weight_terms(values, grads, which):
-        turned = values.reshape(28 * W, 256).astype(F32).T.astype(BF16)
-        column = lax.broadcasted_iota(jnp.int32, (24, W, 256), 1)
-        chosen = jnp.where((column >= 8) & (column < 18), grads[8:32].astype(F32), 0.0)
-        chosen = chosen.reshape(24 * W, 256)
+        turned = narrowed(values, 28, -6).reshape(28 * 16, 256).T.astype(BF16)
+        column = lax.broadcasted_iota(jnp.int32, (24, 16, 256), 1)
         for j in range(3):
-            shifted = chosen
-            if j != 1:
-                shifted = pltpu.roll(chosen, (24 * W + 2 * (j - 1)) % (24 * W), 0)
-            mine[j, 8:32] = shifted.reshape(24, W, 256).astype(BF16)
+            kept = (column >= 2 * j) & (column < 2 * j + 10)
+            shifted = narrowed(grads[8:32], 24, 2 * j - 8)
+            mine[j, 8:32] = jnp.where(kept, shifted, 0.0).astype(BF16)
+
         def step(i, _):
             for j in range(3):
-                rows = mine[j, pl.ds(8 - 2 * i, 28)].reshape(28 * W, 256)
+                rows = mine[j, pl.ds(8 - 2 * i, 28)].reshape(28 * 16, 256)
                 got = jnp.dot(turned, rows, preferred_element_type=F32).astype(BF16)
                 got = got.reshape(8, 2, 16, 256)
                 for side in range(2):
@@ -200,8 +240,8 @@
         lax.fori_loop(0, 3, step, 0)
 
     for j in range(3):
-        mine[j, :8] = jnp.zeros((8, W, 256), BF16)
-        mine[j, 32:] = jnp.zeros((8, W, 256), BF16)
+        mine[j, :8] = jnp.zeros((8, 16, 256), BF16)
+        mine[j, 32:] = jnp.zeros((8, 16, 256), BF16)
     weight_terms(hidden[6:34], second, 1)
     weight_terms(acts[pl.ds(6 + 24 * core, 28), :W, :], first, 0)
     send[...] = terms[1 - core].reshape(2, 8, 288, 128)
@@ -224,34 +264,49 @@
     for j in range(16):
         term = pieces[j, :288, :].astype(F32)
         total = term if total is None else total + term
-    total = jnp.concatenate([total, jnp.zeros((96, 128), F32)], axis=0).T.astype(BF16)
+    total = jnp.concatenate([total, jnp.zeros((96, 128), F32)], axis=0).T
     for z in range(8):
-        windows[z, 48:, :] = total[16 * z : 16 * z + 16]
-        windows[z, :48, 256:] = jnp.zeros((48, 128), BF16)
+        windows[z, 48:64, :] = total[16 * z : 16 * z + 16, :128].astype(BF16)
+        windows[z, 64:80, :] = total[16 * z : 16 * z + 16, 128:256].astype(BF16)
+    lane = lax.broadcasted_iota(jnp.int32, (128, 128), 1)
+    rest = pltpu.roll(total[:, 256:], 96, 1)
     columns[...] = jnp.zeros((256, 128), F32)
     for i in range(3):
         for j in range(16):
             columns[10 * j : 10 * j + 16, :] = pieces[j, 288 + 16 * i : 304 + 16 * i, :].astype(
                 F32
             )
-        turned = columns[...].T.astype(BF16)
+        turned = columns[...].T
         for z in range(8):
-            windows[z, 16 * i : 16 * i + 16, :256] = turned[16 * z : 16 * z + 16]
-
-
-def finish_kernel(scale, at, *rest):
-    pieces, image_out, filters_out, wide = rest
+            windows[z, 16 * i : 16 * i + 16, :] = turned[16 * z : 16 * z + 16, :128].astype(BF16)
+        end = turned[:, 128:]
+        if i:
+            end = pltpu.roll(end, 32 * i, 1)
+        rest = jnp.where((lane >= 32 * i) & (lane < 32 * i + 32), end, rest)
+    for z in range(8):
+        windows[z, 80:, :] = rest[16 * z : 16 * z + 16].astype(BF16)
+
+
+def finish_kernel(scale, at, pieces, image_out, grad_one, grad_two, wide):
     total = None
     for z in range(8):
-        term = pieces[z, 48:, :].astype(F32)
-        total = term if total is None else total + term
-    filters_out[...] = total * scale
+        parts = [pieces[z, k : k + 16, :].astype(F32) for k in (48, 64, 80)]
+        total = parts if total is None else [t + p for t, p in zip(total, parts)]
+    total[2] = pltpu.roll(total[2], 32, 1)
+    total = jnp.concatenate(total, axis=1) * scale
+    for out, at_lane in ((grad_one, 0), (grad_two, 144)):
+        part = total if at_lane == 0 else pltpu.roll(total, 384 - at_lane, 1)
+        out[...] = jnp.concatenate([part[:, :256], jnp.zeros((112, 256), F32)], axis=0).T[:144, :16]
     lane = lax.broadcasted_iota(jnp.int32, (48, 384), 1)
     wide[...] = jnp.zeros((48, 1536), F32)
     for z in range(8):
         base = 160 * z // 128 * 128
         off = 160 * z - base
-        value = pieces[z, :48, :].astype(F32)
+        tail = pieces[z, 80:, :].astype(F32)
+        tail = jnp.concatenate([tail] + [pltpu.roll(tail, 128 - 32 * i, 1) for i in (1, 2)], axis=0)
+        value = jnp.concatenate(
+            [pieces[z, :48, :].astype(F32), tail, jnp.zeros((48, 128), F32)], axis=1
+        )
         if off:
             value = pltpu.roll(value, off, 1)
         wide[:, base : base + 384] = jnp.where(
@@ -276,17 +331,17 @@
     def rows_first(a):
         return jnp.transpose(a, (1, 0, 2)).reshape(48, 1280)
 
-    filters = jnp.concatenate(
-        [jnp.transpose(f, (2, 1, 0)).reshape(16, 144) for f in (filter_one, filter_two)]
-        + [jnp.zeros((16, 96), BF16)],
-        axis=1,
-    )
+    filters = [jnp.transpose(f, (1, 0, 2)).reshape(144, 16) for f in (filter_one, filter_two)]
     pieces = call(
         windows_kernel,
         shape((8, 64, 384)),
-        [pltpu.VMEM((48, 1792), F32), pltpu.VMEM((48, 1792), F32)],
-        [rows_first(image), rows_first(cotangent), filters],
-        at,
+        [pltpu.VMEM((48, 1792), F32)] * 2
+        + [pltpu.VMEM((48, 1280), BF16)] * 2
+        + [pltpu.VMEM((144, 16), BF16)] * 2
+        + [pltpu.SemaphoreType.DMA((4,))],
+        [rows_first(image), rows_first(cotangent), *filters],
+        at,
+        space=pltpu.HBM,
     )
     pieces = call(
         turn_kernel,
@@ -306,7 +361,7 @@
             pltpu.VMEM((40, W, 256), BF16),
             pltpu.VMEM((40, W, 256), BF16),
             pltpu.VMEM((40, W, 256), BF16),
-            pltpu.VMEM((3, 40, W, 256), BF16),
+            pltpu.VMEM((3, 40, 16, 256), BF16),
             pltpu.VMEM((2, 2, 8, 18, 16, 128), BF16),
             pltpu.VMEM((24, 16, 256), BF16),
         ],
@@ -323,21 +378,20 @@
     )
     pieces = call(
         regroup_kernel,
-        shape((8, 64, 384)),
+        shape((8, 96, 128)),
         [pltpu.VMEM((256, 128), F32)],
         [exchanged(pieces, TORUS)],
         at,
     )
-    image_grad, filter_grads = call(
+    image_grad, *filter_grads = call(
         functools.partial(finish_kernel, scale),
-        [shape((48, 1280)), shape((16, 384), F32)],
+        [shape((48, 1280)), shape((144, 16), F32), shape((144, 16), F32)],
         [pltpu.VMEM((48, 1536), F32)],
         [exchanged(pieces, "z")],
         at,
     )
     grad_one, grad_two = (
-        jnp.transpose(filter_grads[:, 144 * k : 144 * k + 144].reshape(16, 9, 16), (2, 1, 0))
-        for k in range(2)
+        jnp.transpose(g.reshape(9, 16, 16), (1, 0, 2)) for g in filter_grads
     )
     return jnp.transpose(image_grad.reshape(3, 16, 1280), (1, 0, 2)), grad_one, grad_two
 

time: 125 us -> 117 us (0.936); the launches traced: 123 us -> 116 us
  blocking collectives: 92.7 us -> 88.6 us
  local copies, waits for them, and re-layouts: 5.19 us -> 3.42 us
    all_to_all x4, blocking collectives: 92.7 us -> 88.6 us  [exchanged(): return lax.all_to_all(array, axes, split_axis=0, concat_axis=0, tiled=True)]
    reshape x2 -> x0, local copies, waits for them, and re-layouts: 1.66 us -> none  [local(): jnp.transpose(f, (2, 1, 0)).reshape(16, 144)]
    slice x3 -> x0, local copies, waits for them, and re-layouts: 1.54 us -> none  [local(): filter_grads[:, 144 * k:144 * k + 144].reshape(16, 9, 16)]
    unnamed x4 -> x8, local copies, waits for them, and re-layouts: 1.81 us -> 3.34 us
where the time goes in v1:
time: 117 us; the launch traced here: 116 us
  blocking collectives  88.6 us (76%)
  Pallas kernels  16.7 us (14%)
  waiting for transfers between devices  6.17 us (5%)
  local copies, waits for them, and re-layouts  3.42 us (3%)
    all_to_all x4, blocking collectives, exchanged(): return lax.all_to_all(array, axes, split_axis=0, concat_axis=0, tiled=True)  88.6 us
    pallas_call x6, Pallas kernels, call(): pl.pallas_call(kernel, out_shape=outs, in_specs=[pl.BlockSpec(memory_spac...  16.7 us
    ppermute x3, waiting for transfers between devices, swapped(): return lax.ppermute(array, 'core', [(0, 1), (1, 0)])  6.17 us
    unnamed x8, local copies, waits for them, and re-layouts  3.34 us
  transfers between devices with their start and end apart: 3, of which 2 were waited for; matrix products, arithmetic and copies ran while one was open for 0% of the time, Pallas kernels for 0%

profile of v1, /device:TPU:8, one launch (start us, length us, event | category | flops | bytes accessed | tf_op | source)
XLA Modules:
  0.0 116.2 jit_solution(15745945643593952945)
XLA Ops:
  0.6 0.1 stack.23.at
  0.7 0.0 copy-start
  0.7 0.9 copy-done
  1.6 0.0 copy-start.1
  1.6 0.9 copy-done.1
  2.5 0.0 copy-start.2
  2.5 0.8 copy-done.2
  3.3 0.8 copy-done.3
  4.1 1.2 %shard_map.67 = bf16[8,64,384]{2,1,0:T(8,128)(2,1)S(1)} custom-call(s32[5]{0:T(128)S(1)} %stack.23.at, bf16[48,1280]{1,0:T(8,128)(2,1)S(1)} %bitcast.26, bf16[48,1280]{1,0:T(8,128)(2,1)S(1)} %bitcast.27, bf16[144,16]{1,0:T(8,128)(2,1)S(1)} %bitcast.28, bf16[144,16]{1,0:T(8,128)(2,1)S(1)} %bitcast.29), custom_call_target="tpu_custom_call" | custom-call | tf_op jit(solution)/shard_map/pallas_call | solution.py:23
  5.3 22.9 %all_to_all.20.rest_0_ = bf16[8,64,384]{2,1,0:T(8,128)(2,1)S(1)} all-to-all(bf16[8,64,384]{2,1,0:T(8,128)(2,1)S(1)} %shard_map.67), channel_id=1, replica_groups=mesh['yh'=2,'z'=8,'yl'=2,'x'=4,'core'=2] {'z'}, dimensions={0} | all-to-all | bytes 786432 | tf_op jit(solution)/shard_map/all_to_all | solution.py:319
  28.2 1.0 shard_map.68
  29.2 29.5 %all_to_all.21.rest_0_ = bf16[16,432,128]{2,1,0:T(8,128)(2,1)S(1)} all-to-all(bf16[16,432,128]{2,1,0:T(8,128)(2,1)S(1)} %shard_map.68), channel_id=1, replica_groups=mesh['yh'=2,'z'=8,'yl'=2,'x'=4,'core'=2] {'yh','yl','x'}, dimensions={0} | all-to-all | bytes 3538944 | tf_op jit(solution)/shard_map/all_to_all | solution.py:319
  58.7 0.0 collective-permute-start
  58.7 3.7 %collective-permute-done.rest_1_ = bf16[16,432,128]{2,1,0:T(8,128)(2,1)S(1)} collective-permute-done((bf16[16,432,128]{2,1,0:T(8,128)(2,1)S(1)}, bf16[16,432,128]{2,1,0:T(8,128)(2,1)S(1)}, u32[]{:S(2)}, u32[]{:S(2)}) %collective-permute-start) | collective-permute-done | bytes 1769504 | tf_op jit(solution)/shard_map/ppermute | solution.py:323
  62.4 11.1 %shard_map.69 = (bf16[2,8,288,128]{3,2,1,0:T(8,128)(2,1)S(1)}, bf16[2,8,288,128]{3,2,1,0:T(8,128)(2,1)S(1)}, bf16[2,4,48,128]{3,2,1,0:T(8,128)(2,1)S(1)}, bf16[2,4,48,128]{3,2,1,0:T(8,128)(2,1)S(1)}) custom-call(s32[5]{0:T(128)S(1)} %stack.23.at, bf16[16,432,128]{2,1,0:T(8,128)(2,1)S(1)} %all_to_all.21.rest_0_, ...), custom_call_target="tpu_custom_call" | custom-call | tf_op jit(solution)/shard_map/pallas_call | solution.py:23
  73.5 0.2 collective-permute-start.1
  73.7 0.4 collective-permute-start.2
  74.1 2.5 %collective-permute-done.2.image_got = bf16[2,4,48,128]{3,2,1,0:T(8,128)(2,1)S(1)} collective-permute-done((bf16[2,4,48,128]{3,2,1,0:T(8,128)(2,1)S(1)}, bf16[2,4,48,128]{3,2,1,0:T(8,128)(2,1)S(1)}, u32[]{:S(2)}, u32[]{:S(2)}) %collective-permute-start.2) | collective-permute-done | bytes 98336 | tf_op jit(solution)/shard_map/ppermute | solution.py:323
  76.5 0.0 collective-permute-done.1.got
  76.5 0.8 shard_map.70
  77.4 24.1 %all_to_all.22.rest_0_ = bf16[16,336,128]{2,1,0:T(8,128)(2,1)S(1)} all-to-all(bf16[16,336,128]{2,1,0:T(8,128)(2,1)S(1)} %shard_map.70), channel_id=1, replica_groups=mesh['yh'=2,'z'=8,'yl'=2,'x'=4,'core'=2] {'yh','yl','x'}, dimensions={0} | all-to-all | bytes 2752512 | tf_op jit(solution)/shard_map/all_to_all | solution.py:319
  101.4 1.1 shard_map.71
  102.5 12.2 %all_to_all.23.pieces = bf16[8,96,128]{2,1,0:T(8,128)(2,1)S(1)} all-to-all(bf16[8,96,128]{2,1,0:T(8,128)(2,1)S(1)} %shard_map.71), channel_id=1, replica_groups=mesh['yh'=2,'z'=8,'yl'=2,'x'=4,'core'=2] {'z'}, dimensions={0} | all-to-all | bytes 393216 | tf_op jit(solution)/shard_map/all_to_all | solution.py:319
  114.7 1.5 %shard_map.72 = (bf16[48,1280]{1,0:T(8,128)(2,1)}, f32[144,16]{1,0:T(8,128)}, f32[144,16]{1,0:T(8,128)}) custom-call(s32[5]{0:T(128)S(1)} %stack.23.at, bf16[8,96,128]{2,1,0:T(8,128)(2,1)S(1)} %all_to_all.23.pieces), custom_call_target="tpu_custom_call" | custom-call | tf_op jit(solution)/shard_map/pallas_call | solution.py:23
  (1 shorter events, 0.0 us)
Async XLA Ops:
  0.7 0.9 copy-start
  1.6 0.9 copy-start.1
  2.5 0.8 copy-start.2
  3.3 0.8 copy-start.3
  58.7 3.7 %collective-permute-start = (bf16[16,432,128]{2,1,0:T(8,128)(2,1)S(1)}, bf16[16,432,128]{2,1,0:T(8,128)(2,1)S(1)}, u32[]{:S(2)}, u32[]{:S(2)}) collective-permute-start(bf16[16,432,128]{2,1,0:T(8,128)(2,1)S(1)} %all_to_all.21.rest_0_), channel_id=1, source_target_pairs={{0,1},{1,0},{2,3},{3,2},{4,5},{5,4},{6,7},{7,6},{8,9},{9,8},{10,11... | collective-permute-start | bytes 5308424 | tf_op jit(solution)/shard_map/ppermute | solution.py:323
  73.5 3.1 %collective-permute-start.1 = (bf16[2,8,288,128]{3,2,1,0:T(8,128)(2,1)S(1)}, bf16[2,8,288,128]{3,2,1,0:T(8,128)(2,1)S(1)}, u32[]{:S(2)}, u32[]{:S(2)}) collective-permute-start(bf16[2,8,288,128]{3,2,1,0:T(8,128)(2,1)S(1)} %get-tuple-element.11), channel_id=1, source_target_pairs={{0,1},{1,0},{2,3},{3,2},{4,5},{5,4},{6,7},{7,6},{8,9},{9,8},{10,11... | collective-permute-start | bytes 3538952 | tf_op jit(solution)/shard_map/ppermute | solution.py:323
  73.7 2.9 %collective-permute-start.2 = (bf16[2,4,48,128]{3,2,1,0:T(8,128)(2,1)S(1)}, bf16[2,4,48,128]{3,2,1,0:T(8,128)(2,1)S(1)}, u32[]{:S(2)}, u32[]{:S(2)}) collective-permute-start(bf16[2,4,48,128]{3,2,1,0:T(8,128)(2,1)S(1)} %get-tuple-element.13), channel_id=1, source_target_pairs={{0,1},{1,0},{2,3},{3,2},{4,5},{5,4},{6,7},{7,6},{8,9},{9,8},{10,11... | collective-permute-start | bytes 294920 | tf_op jit(solution)/shard_map/ppermute | solution.py:323

commit v2 on v1

--- a/solution.py
+++ b/solution.py
@@ -9,6 +9,7 @@
 from jax.sharding import Mesh
 from jax.sharding import PartitionSpec as P
 
+
 AXES = ("yh", "z", "yl", "x", "core")
 CHAN = ("yh", "z")
 STRIP = ("yl", "x", "core")
@@ -19,14 +20,15 @@
 W = 32
 
 
-def call(kernel, outs, scratch, args, prefetch, room=10, space=pltpu.VMEM):
+def call(kernel, outs, scratch, args, prefetch, room=10, space=None, cost=10**7):
     return pl.pallas_call(
         kernel,
         out_shape=outs,
         in_specs=[pl.BlockSpec(memory_space=pltpu.SMEM)]
-        + [pl.BlockSpec(memory_space=space)] * len(args),
+        + [pl.BlockSpec(memory_space=s) for s in (space or [pltpu.VMEM] * len(args))],
         out_specs=jax.tree.map(lambda _: pl.BlockSpec(memory_space=pltpu.VMEM), outs),
         scratch_shapes=scratch,
+        cost_estimate=pl.CostEstimate(flops=cost, bytes_accessed=10**6, transcendentals=0),
         compiler_params=pltpu.CompilerParams(vmem_limit_bytes=room * 2**20),
     )(prefetch, *args)
 
@@ -79,7 +81,7 @@
 
 
 def turn_kernel(at, *rest):
-    held, outs, turned, chunk = rest
+    held, outs, later, turned, chunk = rest
     for i in range(3):
         turned[...] = held[:, 16 * i : 16 * i + 16, :].reshape(128, 384).astype(F32).T
         for j in range(16):
@@ -88,18 +90,83 @@
             outs[j, 48 * i : 48 * i + 48, :] = chunk[...].astype(BF16)
     filters = held[:, 48:, :].reshape(128, 384).astype(F32).T[:288].astype(BF16)
     for j in range(16):
-        outs[j, 144:, :] = filters
+        outs[j, 144:, :] = filters[:144]
+        later[j] = filters[144:]
 
 
 def sigmoid(v):
     return 0.5 + 0.5 * jnp.tanh(0.5 * v)
 
 
-def conv_kernel(at, *rest):
-    own, other = rest[:2]
-    send, keep, image_send, image_keep = rest[2:6]
-    acts, wide, pre, hidden, second, first, mine, terms, image_rows = rest[6:]
-    y, x, core, z = at[2], at[3], at[4], at[1]
+def tap(wide, i, j):
+    return wide[3 * i + j].reshape(256, 256)
+
+
+def ahead(source, wide, start, rows):
+    band = jnp.concatenate(
+        [source[pl.ds(start + 2 * i - 2, rows), :W, :] for i in range(3)], axis=-1
+    ).reshape(rows * W, 768)
+    total = None
+    for j in range(3):
+        weights = jnp.concatenate([tap(wide, i, j) for i in range(3)], axis=0)
+        term = jnp.dot(band, weights, preferred_element_type=F32)
+        if j != 1:
+            term = pltpu.roll(term, (rows * W - 2 * (j - 1)) % (rows * W), 0)
+        total = term if total is None else total + term
+    return total.reshape(rows, W, 256)
+
+
+def backward(source, wide, start, rows):
+    band = jnp.concatenate(
+        [source[pl.ds(start - 2 * i + 2, rows), :, :] for i in range(3)], axis=-1
+    ).reshape(rows * W, 768)
+    total = None
+    for j in range(3):
+        weights = jnp.concatenate([tap(wide, i, j) for i in range(3)], axis=1)
+        term = lax.dot_general(
+            band, weights, (((1,), (1,)), ((), ())), preferred_element_type=F32
+        )
+        if j != 1:
+            term = pltpu.roll(term, (rows * W + 2 * (j - 1)) % (rows * W), 0)
+        total = term if total is None else total + term
+    return total.reshape(rows, W, 256)
+
+
+def slope(v):
+    s = sigmoid(v)
+    return s * (1.0 + v * (1.0 - s))
+
+
+def each(start, count, rows, body):
+    def step(k, _):
+        body(start + k * rows)
+        return 0
+
+    lax.fori_loop(0, count, step, 0)
+
+
+def cleared(at, target):
+    z, y, x, core = (at[k] for k in range(1, 5))
+
+    @pl.when(core == 0)
+    def _():
+        target[:8] = jnp.zeros((8, W, 256), BF16)
+
+    @pl.when(core == 1)
+    def _():
+        target[32:] = jnp.zeros((8, W, 256), BF16)
+
+    @pl.when((z == 0) & (y + x == 0))
+    def _():
+        target[:, :8, :] = jnp.zeros((40, 8, 256), BF16)
+
+    @pl.when((z == 7) & (y + x == 6))
+    def _():
+        target[:, 18:, :] = jnp.zeros((40, 14, 256), BF16)
+
+
+def first_kernel(at, own, other, acts, wide, pre, hidden):
+    core = at[4]
     acts[:8] = jnp.zeros((8, 48, 256), BF16)
     acts[56:] = jnp.zeros((8, 48, 256), BF16)
     for pieces, side in ((own, core), (other, 1 - core)):
@@ -108,100 +175,58 @@
             strip = 2 * (j % 8) + side
             lanes = slice(half * 128, half * 128 + 128)
             acts[pl.ds(3 * strip + 8, 3), :, lanes] = pieces[j, :144, :].reshape(3, 48, 128)
-            wide[:, strip, :, lanes] = pieces[j, 144:, :].reshape(18, 16, 128)
-
-    at_left = (z == 0) & (y + x == 0)
-    at_right = (z == 7) & (y + x == 6)
-
-    def cleared(target):
-        @pl.when(core == 0)
-        def _():
-            target[:8] = jnp.zeros((8, W, 256), BF16)
-
-        @pl.when(core == 1)
-        def _():
-            target[32:] = jnp.zeros((8, W, 256), BF16)
-
-        @pl.when(at_left)
-        def _():
-            target[:, :8, :] = jnp.zeros((40, 8, 256), BF16)
-
-        @pl.when(at_right)
-        def _():
-            target[:, 18:, :] = jnp.zeros((40, 14, 256), BF16)
-
-    def tap(which, i, j):
-        return wide[9 * which + 3 * i + j].reshape(256, 256)
-
-    def ahead(source, start, rows, which):
-        band = jnp.concatenate(
-            [source[pl.ds(start + 2 * i - 2, rows), :W, :] for i in range(3)], axis=-1
-        ).reshape(rows * W, 768)
-        total = None
-        for j in range(3):
-            weights = jnp.concatenate([tap(which, i, j) for i in range(3)], axis=0)
-            term = jnp.dot(band, weights, preferred_element_type=F32)
-            if j != 1:
-                term = pltpu.roll(term, (rows * W - 2 * (j - 1)) % (rows * W), 0)
-            total = term if total is None else total + term
-        return total.reshape(rows, W, 256)
-
-    def backward(source, start, rows, which):
-        band = jnp.concatenate(
-            [source[pl.ds(start - 2 * i + 2, rows), :, :] for i in range(3)], axis=-1
-        ).reshape(rows * W, 768)
-        total = None
-        for j in range(3):
-            weights = jnp.concatenate([tap(which, i, j) for i in range(3)], axis=1)
-            term = lax.dot_general(
-                band, weights, (((1,), (1,)), ((), ())), preferred_element_type=F32
-            )
-            if j != 1:
-                term = pltpu.roll(term, (rows * W + 2 * (j - 1)) % (rows * W), 0)
-            total = term if total is None else total + term
-        return total.reshape(rows, W, 256)
-
-    def slope(v):
-        s = sigmoid(v)
-        return s * (1.0 + v * (1.0 - s))
-
-    def each(start, count, rows, body):
-        def step(k, _):
-            body(start + k * rows)
-            return 0
-
-        lax.fori_loop(0, count, step, 0)
+            wide[:, strip, :, lanes] = pieces[j, 144:, :].reshape(9, 16, 128)
 
     def first_step(start):
-        rows = 12
-        value = ahead(acts, start + 24 * core, rows, 0)
-        pre[pl.ds(start, rows)] = value
-        hidden[pl.ds(start, rows)] = (value * sigmoid(value)).astype(BF16)
+        value = ahead(acts, wide, start + 24 * core, 12)
+        pre[pl.ds(start, 12)] = value
+        hidden[pl.ds(start, 12)] = (value * sigmoid(value)).astype(BF16)
 
     each(2, 3, 12, first_step)
-    cleared(hidden)
+    cleared(at, hidden)
+
+
+def conv_kernel(at, own, other, *rest):
+    state, (send, keep, image_send, image_keep) = rest[:4], rest[4:8]
+    wide, second, first, mine, terms, image_rows = rest[8:14]
+    held, arrived = rest[14:18], rest[18]
+    copies = [
+        pltpu.make_async_copy(a, b, arrived.at[k]) for k, (a, b) in enumerate(zip(state, held))
+    ]
+    for copy in copies:
+        copy.start()
+    acts, wide_one, pre, hidden = held
+    core = at[4]
+    for pieces, side in ((own, core), (other, 1 - core)):
+        for j in range(16):
+            half = j // 8
+            strip = 2 * (j % 8) + side
+            wide[:, strip, :, half * 128 : half * 128 + 128] = pieces[j].reshape(9, 16, 128)
+
+    for copy in copies:
+        copy.wait()
 
     def second_step(start):
         rows = 16
-        value = ahead(hidden, start, rows, 1)
+        value = ahead(hidden, wide, start, rows)
         got = acts[pl.ds(start + 24 * core, rows), 16:, :].astype(F32).reshape(rows * W, 256)
         got = pltpu.roll(got, rows * W - 6, 0).reshape(rows, W, 256)
         second[pl.ds(start, rows)] = (got * slope(value)).astype(BF16)
 
     each(4, 2, 16, second_step)
-    cleared(second)
+    cleared(at, second)
 
     def third_step(start):
         rows = 14
-        value = backward(second, start, rows, 1)
+        value = backward(second, wide, start, rows)
         first[pl.ds(start, rows)] = (value * slope(pre[pl.ds(start, rows)])).astype(BF16)
 
     each(6, 2, 14, third_step)
-    cleared(first)
+    cleared(at, first)
 
     def fourth_step(start):
         rows = 12
-        value = backward(first, start, rows, 0)
+        value = backward(first, wide_one, start, rows)
         image_rows[pl.ds(start - 8, rows)] = value[:, 8:24, :].astype(BF16)
 
     each(8, 2, 12, fourth_step)
@@ -341,33 +366,50 @@
         + [pltpu.SemaphoreType.DMA((4,))],
         [rows_first(image), rows_first(cotangent), *filters],
         at,
-        space=pltpu.HBM,
-    )
-    pieces = call(
+        room=63,
+        space=[pltpu.HBM] * 4,
+    )
+    early, late = call(
         turn_kernel,
-        shape((16, 432, 128)),
+        [shape((16, 288, 128)), shape((16, 144, 128))],
         [pltpu.VMEM((384, 128), F32), pltpu.VMEM((48, 128), F32)],
         [exchanged(pieces, "z")],
         at,
     )
-    pieces = exchanged(pieces, TORUS)
+    early = exchanged(early, TORUS)
+    late = exchanged(late, TORUS)
+    early_other = swapped(early)
+    state = call(
+        first_kernel,
+        [
+            shape((64, 48, 256)),
+            shape((9, 16, 16, 256)),
+            shape((40, W, 256), F32),
+            shape((40, W, 256)),
+        ],
+        [],
+        [early, early_other],
+        at,
+        cost=2 * 10**9,
+    )
     send, keep, image_send, image_keep = call(
         conv_kernel,
         [shape((2, 8, 288, 128))] * 2 + [shape((2, 4, 48, 128))] * 2,
         [
-            pltpu.VMEM((64, 48, 256), BF16),
-            pltpu.VMEM((18, 16, 16, 256), BF16),
-            pltpu.VMEM((40, W, 256), F32),
-            pltpu.VMEM((40, W, 256), BF16),
+            pltpu.VMEM((9, 16, 16, 256), BF16),
             pltpu.VMEM((40, W, 256), BF16),
             pltpu.VMEM((40, W, 256), BF16),
             pltpu.VMEM((3, 40, 16, 256), BF16),
             pltpu.VMEM((2, 2, 8, 18, 16, 128), BF16),
             pltpu.VMEM((24, 16, 256), BF16),
+            *(pltpu.VMEM(a.shape, a.dtype) for a in state),
+            pltpu.SemaphoreType.DMA((4,)),
         ],
-        [pieces, swapped(pieces)],
-        at,
-        28,
+        [late, swapped(late), *(pltpu.with_memory_space_constraint(a, pltpu.HBM) for a in state)],
+        at,
+        room=24,
+        space=[pltpu.VMEM] * 2 + [pltpu.HBM] * 4,
+        cost=6 * 10**9,
     )
     pieces = call(
         scatter_kernel,

time: 117 us -> 130 us (1.11)
  blocking collectives: 88.6 us -> 98.3 us
  Pallas kernels: 16.7 us -> 21.2 us
  waiting for transfers between devices: 6.17 us -> 2.52 us
  local copies, waits for them, and re-layouts: 3.42 us -> 4.75 us
    all_to_all x4 -> x5, blocking collectives: 88.6 us -> 98.3 us  [exchanged(): return lax.all_to_all(array, axes, split_axis=0, concat_axis=0, tiled=True)]
    pallas_call x6 -> x7, Pallas kernels: 16.7 us -> 21.2 us  [call(): pl.pallas_call(kernel, out_shape=outs, in_specs=[pl.BlockSpec(memory_spac...]
    ppermute x3 -> x4, waiting for transfers between devices: 6.17 us -> 2.52 us  [swapped(): return lax.ppermute(array, 'core', [(0, 1), (1, 0)])]
    unnamed x8 -> x10, local copies, waits for them, and re-layouts: 3.34 us -> 4.09 us
  transfers between devices with their start and end apart: 3 -> 4, of which waited for: 2 -> 1; matrix products, arithmetic and copies ran while one was open for 0% -> 0% of each run, Pallas kernels for 0% -> 2%
where the time goes in v2:
time: 130 us; the launch traced here: 128 us
  blocking collectives  98.3 us (76%)
  Pallas kernels  21.2 us (16%)
  local copies, waits for them, and re-layouts  4.75 us (4%)
  waiting for transfers between devices  2.52 us (2%)
    all_to_all x5, blocking collectives, exchanged(): return lax.all_to_all(array, axes, split_axis=0, concat_axis=0, tiled=True)  98.3 us
    pallas_call x7, Pallas kernels, call(): pl.pallas_call(kernel, out_shape=outs, in_specs=[pl.BlockSpec(memory_spac...  21.2 us
    unnamed x10, local copies, waits for them, and re-layouts  4.09 us
  transfers between devices with their start and end apart: 4, of which 1 were waited for; matrix products, arithmetic and copies ran while one was open for 0% of the time, Pallas kernels for 2%

profile of v2, /device:TPU:8, one launch (start us, length us, event | category | flops | bytes accessed | tf_op | source)
XLA Modules:
  0.0 128.2 jit_solution(231321357264811033)
XLA Ops:
  0.6 0.7 stack.23.at
  1.3 2.8 %shard_map.67 = bf16[8,64,384]{2,1,0:T(8,128)(2,1)} custom-call(s32[5]{0:T(128)} %stack.23.at, bf16[48,1280]{1,0:T(8,128)(2,1)} %bitcast.26, bf16[48,1280]{1,0:T(8,128)(2,1)} %bitcast.27, bf16[144,16]{1,0:T(8,128)(2,1)} %bitcast.28, bf16[144,16]{1,0:T(8,128)(2,1)} %bitcast.29), custom_call_target="tpu_custom_call" | custom-call | flops 10000000 | bytes 1000000 | tf_op jit(solution)/shard_map/pallas_call | solution.py:24
  4.1 23.2 %all_to_all.25.rest_0_ = bf16[8,64,384]{2,1,0:T(8,128)(2,1)S(1)} all-to-all(bf16[8,64,384]{2,1,0:T(8,128)(2,1)} %shard_map.67), channel_id=1, replica_groups=mesh['yh'=2,'z'=8,'yl'=2,'x'=4,'core'=2] {'z'}, dimensions={0} | all-to-all | bytes 786432 | tf_op jit(solution)/shard_map/all_to_all | solution.py:344
  27.2 1.0 shard_map.68
  28.2 23.1 %all_to_all.26.own = bf16[16,288,128]{2,1,0:T(8,128)(2,1)S(1)} all-to-all(bf16[16,288,128]{2,1,0:T(8,128)(2,1)S(1)} %get-tuple-element.17), channel_id=1, replica_groups=mesh['yh'=2,'z'=8,'yl'=2,'x'=4,'core'=2] {'yh','yl','x'}, dimensions={0} | all-to-all | bytes 2359296 | tf_op jit(solution)/shard_map/all_to_all | solution.py:344
  51.3 0.0 collective-permute-start.1
  51.4 16.3 %all_to_all.27.own = bf16[16,144,128]{2,1,0:T(8,128)(2,1)S(1)} all-to-all(bf16[16,144,128]{2,1,0:T(8,128)(2,1)S(1)} %get-tuple-element.16), channel_id=1, replica_groups=mesh['yh'=2,'z'=8,'yl'=2,'x'=4,'core'=2] {'yh','yl','x'}, dimensions={0} | all-to-all | bytes 1179648 | tf_op jit(solution)/shard_map/all_to_all | solution.py:344
  67.6 0.0 collective-permute-start
  67.7 0.0 collective-permute-done.1.other
  67.7 3.0 %shard_map.69 = (bf16[64,48,256]{2,1,0:T(8,128)(2,1)S(1)}, bf16[9,16,16,256]{3,2,1,0:T(8,128)(2,1)S(1)}, f32[40,32,256]{2,1,0:T(8,128)S(1)}, bf16[40,32,256]{2,1,0:T(8,128)(2,1)S(1)}) custom-call(s32[5]{0:T(128)S(1)} %copy-done, bf16[16,288,128]{2,1,0:T(8,128)(2,1)S(1)} %all_to_all.26.own, bf16[16,288,128]{2,1,0:T(8,128)(2,1)S(1)} %collective-permute-done.1.other), custom_call_target="tpu_custom_call" | custom-call | flops 2000000000 | bytes 1000000 | tf_op jit(solution)/shard_map/pallas_call | solution.py:24
  70.7 1.2 copy-done.1
  71.8 1.1 copy-done.2
  72.9 1.0 copy-done.3
  73.9 0.8 copy-done.4
  74.7 0.0 collective-permute-done.other
  74.7 11.0 %shard_map.70 = (bf16[2,8,288,128]{3,2,1,0:T(8,128)(2,1)S(1)}, bf16[2,8,288,128]{3,2,1,0:T(8,128)(2,1)S(1)}, bf16[2,4,48,128]{3,2,1,0:T(8,128)(2,1)S(1)}, bf16[2,4,48,128]{3,2,1,0:T(8,128)(2,1)S(1)}) custom-call(s32[5]{0:T(128)S(1)} %copy-done, bf16[16,144,128]{2,1,0:T(8,128)(2,1)S(1)} %all_to_all.27.own, ...), custom_call_target="tpu_custom_call" | custom-call | flops 6000000000 | bytes 1000000 | tf_op jit(solution)/shard_map/pallas_call | solution.py:24
  85.8 0.6 collective-permute-start.2
  86.3 0.1 collective-permute-start.3
  86.4 2.5 %collective-permute-done.3.image_got = bf16[2,4,48,128]{3,2,1,0:T(8,128)(2,1)S(1)} collective-permute-done((bf16[2,4,48,128]{3,2,1,0:T(8,128)(2,1)S(1)}, bf16[2,4,48,128]{3,2,1,0:T(8,128)(2,1)S(1)}, u32[]{:S(2)}, u32[]{:S(2)}) %collective-permute-start.3) | collective-permute-done | bytes 98336 | tf_op jit(solution)/shard_map/ppermute | solution.py:348
  89.0 0.8 shard_map.71
  89.8 23.4 %all_to_all.28.rest_0_ = bf16[16,336,128]{2,1,0:T(8,128)(2,1)S(1)} all-to-all(bf16[16,336,128]{2,1,0:T(8,128)(2,1)S(1)} %shard_map.71), channel_id=1, replica_groups=mesh['yh'=2,'z'=8,'yl'=2,'x'=4,'core'=2] {'yh','yl','x'}, dimensions={0} | all-to-all | bytes 2752512 | tf_op jit(solution)/shard_map/all_to_all | solution.py:344
  113.2 1.1 shard_map.72
  114.3 12.3 %all_to_all.29.pieces = bf16[8,96,128]{2,1,0:T(8,128)(2,1)S(1)} all-to-all(bf16[8,96,128]{2,1,0:T(8,128)(2,1)S(1)} %shard_map.72), channel_id=1, replica_groups=mesh['yh'=2,'z'=8,'yl'=2,'x'=4,'core'=2] {'z'}, dimensions={0} | all-to-all | bytes 393216 | tf_op jit(solution)/shard_map/all_to_all | solution.py:344
  126.6 1.5 %shard_map.73 = (bf16[48,1280]{1,0:T(8,128)(2,1)}, f32[144,16]{1,0:T(8,128)}, f32[144,16]{1,0:T(8,128)}) custom-call(s32[5]{0:T(128)S(1)} %copy-done, bf16[8,96,128]{2,1,0:T(8,128)(2,1)S(1)} %all_to_all.29.pieces), custom_call_target="tpu_custom_call" | custom-call | flops 10000000 | bytes 1000000 | tf_op jit(solution)/shard_map/pallas_call | solution.py:24
  (7 shorter events, 0.0 us)
Async XLA Ops:
  1.3 25.9 %copy-start = (s32[5]{0:T(128)S(1)}, s32[5]{0:T(128)}, u32[]{:S(2)}) copy-start(s32[5]{0:T(128)} %stack.23.at) | copy-start | bytes 64
  51.3 16.3 %collective-permute-start.1 = (bf16[16,288,128]{2,1,0:T(8,128)(2,1)S(1)}, bf16[16,288,128]{2,1,0:T(8,128)(2,1)S(1)}, u32[]{:S(2)}, u32[]{:S(2)}) collective-permute-start(bf16[16,288,128]{2,1,0:T(8,128)(2,1)S(1)} %all_to_all.26.own), channel_id=1, source_target_pairs={{0,1},{1,0},{2,3},{3,2},{4,5},{5,4},{6,7},{7,6},{8,9},{9,8},{10,11... | collective-permute-start | bytes 3538952 | tf_op jit(solution)/shard_map/ppermute | solution.py:348
  67.6 7.1 %collective-permute-start = (bf16[16,144,128]{2,1,0:T(8,128)(2,1)S(1)}, bf16[16,144,128]{2,1,0:T(8,128)(2,1)S(1)}, u32[]{:S(2)}, u32[]{:S(2)}) collective-permute-start(bf16[16,144,128]{2,1,0:T(8,128)(2,1)S(1)} %all_to_all.27.own), channel_id=1, source_target_pairs={{0,1},{1,0},{2,3},{3,2},{4,5},{5,4},{6,7},{7,6},{8,9},{9,8},{10,11... | collective-permute-start | bytes 1769480 | tf_op jit(solution)/shard_map/ppermute | solution.py:348
  70.6 1.2 copy-start.1
  71.8 1.1 copy-start.2
  72.9 1.0 copy-start.3
  73.9 0.8 copy-start.4
  85.8 3.2 %collective-permute-start.2 = (bf16[2,8,288,128]{3,2,1,0:T(8,128)(2,1)S(1)}, bf16[2,8,288,128]{3,2,1,0:T(8,128)(2,1)S(1)}, u32[]{:S(2)}, u32[]{:S(2)}) collective-permute-start(bf16[2,8,288,128]{3,2,1,0:T(8,128)(2,1)S(1)} %get-tuple-element.23), channel_id=1, source_target_pairs={{0,1},{1,0},{2,3},{3,2},{4,5},{5,4},{6,7},{7,6},{8,9},{9,8},{10,11... | collective-permute-start | bytes 3538952 | tf_op jit(solution)/shard_map/ppermute | solution.py:348
  86.3 2.6 %collective-permute-start.3 = (bf16[2,4,48,128]{3,2,1,0:T(8,128)(2,1)S(1)}, bf16[2,4,48,128]{3,2,1,0:T(8,128)(2,1)S(1)}, u32[]{:S(2)}, u32[]{:S(2)}) collective-permute-start(bf16[2,4,48,128]{3,2,1,0:T(8,128)(2,1)S(1)} %get-tuple-element.25), channel_id=1, source_target_pairs={{0,1},{1,0},{2,3},{3,2},{4,5},{5,4},{6,7},{7,6},{8,9},{9,8},{10,11... | collective-permute-start | bytes 294920 | tf_op jit(solution)/shard_map/ppermute | solution.py:348

commit v3 on v1

--- a/solution.py
+++ b/solution.py
@@ -19,23 +19,26 @@
 W = 32
 
 
-def call(kernel, outs, scratch, args, prefetch, room=10, space=pltpu.VMEM):
+def call(kernel, outs, scratch, args, prefetch=None, room=10, space=pltpu.VMEM):
+    where = [pl.BlockSpec(memory_space=space)] * len(args)
+    if prefetch is not None:
+        where = [pl.BlockSpec(memory_space=pltpu.SMEM)] + where
+        args = [prefetch, *args]
     return pl.pallas_call(
         kernel,
         out_shape=outs,
-        in_specs=[pl.BlockSpec(memory_space=pltpu.SMEM)]
-        + [pl.BlockSpec(memory_space=space)] * len(args),
+        in_specs=where,
         out_specs=jax.tree.map(lambda _: pl.BlockSpec(memory_space=pltpu.VMEM), outs),
         scratch_shapes=scratch,
         compiler_params=pltpu.CompilerParams(vmem_limit_bytes=room * 2**20),
-    )(prefetch, *args)
+    )(*args)
 
 
 def shape(dims, kind=BF16):
     return jax.ShapeDtypeStruct(dims, kind)
 
 
-def windows_kernel(at, *rest):
+def windows_kernel(*rest):
     sources, (windows, image_wide, cotangent_wide), held, arrived = (
         rest[:4],
         rest[4:7],
@@ -78,7 +81,7 @@
         windows[z, 48:, :] = pieces
 
 
-def turn_kernel(at, *rest):
+def turn_kernel(*rest):
     held, outs, turned, chunk = rest
     for i in range(3):
         turned[...] = held[:, 16 * i : 16 * i + 16, :].reshape(128, 384).astype(F32).T
@@ -95,11 +98,33 @@
     return 0.5 + 0.5 * jnp.tanh(0.5 * v)
 
 
+def rolled(value, shift):
+    shift %= value.shape[0]
+    return pltpu.roll(value, shift, 0) if shift else value
+
+
+def tapped(band, wide, shifts, transposed):
+    total = None
+    for j in range(3):
+        taps = [wide[3 * i + j].reshape(256, 256) for i in range(3)]
+        weights = jnp.concatenate(taps, axis=1 if transposed else 0)
+        over = (((1,), (1 if transposed else 0,)), ((), ()))
+        term = lax.dot_general(band, weights, over, preferred_element_type=F32)
+        term = rolled(term, shifts[j])
+        total = term if total is None else total + term
+    return total
+
+
+def silu_slope(v):
+    s = sigmoid(v)
+    return s * (1.0 + v * (1.0 - s))
+
+
 def conv_kernel(at, *rest):
     own, other = rest[:2]
     send, keep, image_send, image_keep = rest[2:6]
-    acts, wide, pre, hidden, second, first, mine, terms, image_rows = rest[6:]
-    y, x, core, z = at[2], at[3], at[4], at[1]
+    acts, wides, pre, hidden, second, first, mine, terms, image_rows = rest[6:]
+    z, y, x, core = (at[k] for k in range(1, 5))
     acts[:8] = jnp.zeros((8, 48, 256), BF16)
     acts[56:] = jnp.zeros((8, 48, 256), BF16)
     for pieces, side in ((own, core), (other, 1 - core)):
@@ -108,103 +133,57 @@
             strip = 2 * (j % 8) + side
             lanes = slice(half * 128, half * 128 + 128)
             acts[pl.ds(3 * strip + 8, 3), :, lanes] = pieces[j, :144, :].reshape(3, 48, 128)
-            wide[:, strip, :, lanes] = pieces[j, 144:, :].reshape(18, 16, 128)
-
-    at_left = (z == 0) & (y + x == 0)
-    at_right = (z == 7) & (y + x == 6)
-
-    def cleared(target):
-        @pl.when(core == 0)
-        def _():
-            target[:8] = jnp.zeros((8, W, 256), BF16)
-
-        @pl.when(core == 1)
-        def _():
-            target[32:] = jnp.zeros((8, W, 256), BF16)
-
-        @pl.when(at_left)
-        def _():
-            target[:, :8, :] = jnp.zeros((40, 8, 256), BF16)
-
-        @pl.when(at_right)
-        def _():
-            target[:, 18:, :] = jnp.zeros((40, 14, 256), BF16)
-
-    def tap(which, i, j):
-        return wide[9 * which + 3 * i + j].reshape(256, 256)
-
-    def ahead(source, start, rows, which):
+            wides[:, strip, :, lanes] = pieces[j, 144:, :].reshape(18, 16, 128)
+    wide_one, wide_two = wides.at[:9], wides.at[9:]
+
+    rows_out = 32 * core
+    hidden[pl.ds(pl.multiple_of(24 * rows_out, 48), 192)] = jnp.zeros((192, 256), BF16)
+    second[pl.ds(pl.multiple_of(24 * rows_out, 48), 192)] = jnp.zeros((192, 256), BF16)
+    first[pl.ds(rows_out, 8)] = jnp.zeros((8, 16, 256), BF16)
+    left = 160 * z + 10 * (4 * y + x) - 8
+
+    def mask(begin, columns):
+        c = lax.broadcasted_iota(jnp.int32, (1, columns, 256), 1) + (left + begin)
+        return ((c >= 0) & (c < 1280)).astype(F32)
+
+    def flat(start, rows):
+        return pl.ds(pl.multiple_of(start * 24, 48), rows * 24)
+
+    mask_24, mask_16 = mask(2, 24), mask(6, 16)
+
+    for k in range(2):
+        rows = (16, 14)[k]
+        start = 8 - 6 * core + 16 * k
         band = jnp.concatenate(
-            [source[pl.ds(start + 2 * i - 2, rows), :W, :] for i in range(3)], axis=-1
+            [acts[pl.ds(start + 24 * core + 2 * i - 2, rows), :W, :] for i in range(3)], axis=-1
         ).reshape(rows * W, 768)
-        total = None
-        for j in range(3):
-            weights = jnp.concatenate([tap(which, i, j) for i in range(3)], axis=0)
-            term = jnp.dot(band, weights, preferred_element_type=F32)
-            if j != 1:
-                term = pltpu.roll(term, (rows * W - 2 * (j - 1)) % (rows * W), 0)
-            total = term if total is None else total + term
-        return total.reshape(rows, W, 256)
-
-    def backward(source, start, rows, which):
-        band = jnp.concatenate(
-            [source[pl.ds(start - 2 * i + 2, rows), :, :] for i in range(3)], axis=-1
-        ).reshape(rows * W, 768)
-        total = None
-        for j in range(3):
-            weights = jnp.concatenate([tap(which, i, j) for i in range(3)], axis=1)
-            term = lax.dot_general(
-                band, weights, (((1,), (1,)), ((), ())), preferred_element_type=F32
-            )
-            if j != 1:
-                term = pltpu.roll(term, (rows * W + 2 * (j - 1)) % (rows * W), 0)
-            total = term if total is None else total + term
-        return total.reshape(rows, W, 256)
-
-    def slope(v):
-        s = sigmoid(v)
-        return s * (1.0 + v * (1.0 - s))
-
-    def each(start, count, rows, body):
-        def step(k, _):
-            body(start + k * rows)
-            return 0
-
-        lax.fori_loop(0, count, step, 0)
-
-    def first_step(start):
-        rows = 12
-        value = ahead(acts, start + 24 * core, rows, 0)
-        pre[pl.ds(start, rows)] = value
-        hidden[pl.ds(start, rows)] = (value * sigmoid(value)).astype(BF16)
-
-    each(2, 3, 12, first_step)
-    cleared(hidden)
-
-    def second_step(start):
-        rows = 16
-        value = ahead(hidden, start, rows, 1)
-        got = acts[pl.ds(start + 24 * core, rows), 16:, :].astype(F32).reshape(rows * W, 256)
-        got = pltpu.roll(got, rows * W - 6, 0).reshape(rows, W, 256)
-        second[pl.ds(start, rows)] = (got * slope(value)).astype(BF16)
-
-    each(4, 2, 16, second_step)
-    cleared(second)
-
-    def third_step(start):
+        value = tapped(band, wide_one, (0, -2, -4), False)
+        pre[pl.ds(start, rows)] = rolled(value, -4).reshape(rows, W, 256)[:, :16, :]
+        value = value.reshape(rows, W, 256)[:, :24, :]
+        value = value * sigmoid(value) * mask_24
+        hidden[flat(start, rows)] = value.reshape(rows * 24, 256).astype(BF16)
+
+    def second_step(k, _):
         rows = 14
-        value = backward(second, start, rows, 1)
-        first[pl.ds(start, rows)] = (value * slope(pre[pl.ds(start, rows)])).astype(BF16)
-
-    each(6, 2, 14, third_step)
-    cleared(first)
-
-    def fourth_step(start):
-        rows = 12
-        value = backward(first, start, rows, 0)
-        image_rows[pl.ds(start - 8, rows)] = value[:, 8:24, :].astype(BF16)
-
-    each(8, 2, 12, fourth_step)
+        start = 8 - 4 * core + rows * k
+        band = jnp.concatenate([hidden[flat(start + 2 * i - 2, rows)] for i in range(3)], axis=-1)
+        value = tapped(band, wide_two, (2, 0, -2), False).reshape(rows, 24, 256)
+        got = acts[pl.ds(start + 24 * core, rows), 16:, :].astype(F32)[:, 8:, :]
+        value = got * silu_slope(value) * mask_24
+        second[flat(start, rows)] = value.reshape(rows * 24, 256).astype(BF16)
+        return 0
+
+    lax.fori_loop(0, 2, second_step, 0)
+
+    start = 8 - 2 * core
+    band = jnp.concatenate([second[flat(start - 2 * i + 2, 26)] for i in range(3)], axis=-1)
+    value = tapped(band, wide_two, (-6, -4, -2), True).reshape(26, 24, 256)[:, :16, :]
+    value = value * silu_slope(pre[pl.ds(start, 26)]) * mask_16
+    first[pl.ds(start, 26)] = value.astype(BF16)
+
+    band = jnp.concatenate([first[10 - 2 * i : 34 - 2 * i] for i in range(3)], axis=-1)
+    value = tapped(band.reshape(384, 768), wide_one, (-4, -2, 0), True)
+    image_rows[...] = value.reshape(24, 16, 256).astype(BF16)
     for side, out in ((1 - core, image_send), (core, image_keep)):
         for k in range(4):
             for half in range(2):
@@ -212,17 +191,16 @@
                     pl.ds(6 * k + 3 * side, 3), :, 128 * half : 128 * half + 128
                 ].reshape(48, 128)
 
-    def narrowed(values, rows, shift):
-        flat = values.astype(F32).reshape(rows * W, 256)
-        flat = pltpu.roll(flat, (rows * W + shift) % (rows * W), 0)
-        return flat.reshape(rows, W, 256)[:, :16, :]
-
-    def weight_terms(values, grads, which):
-        turned = narrowed(values, 28, -6).reshape(28 * 16, 256).T.astype(BF16)
+    def narrowed(values, columns, shift):
+        rows = values.shape[0] // columns
+        return rolled(values.astype(F32), shift).reshape(rows, columns, 256)[:, :16, :]
+
+    def weight_terms(values, grads, columns, which):
+        turned = values.reshape(28 * 16, 256).T.astype(BF16)
         column = lax.broadcasted_iota(jnp.int32, (24, 16, 256), 1)
         for j in range(3):
             kept = (column >= 2 * j) & (column < 2 * j + 10)
-            shifted = narrowed(grads[8:32], 24, 2 * j - 8)
+            shifted = narrowed(grads, columns, 2 * j - 2 - (4 if columns == 24 else 0))
             mine[j, 8:32] = jnp.where(kept, shifted, 0.0).astype(BF16)
 
         def step(i, _):
@@ -242,8 +220,9 @@
     for j in range(3):
         mine[j, :8] = jnp.zeros((8, 16, 256), BF16)
         mine[j, 32:] = jnp.zeros((8, 16, 256), BF16)
-    weight_terms(hidden[6:34], second, 1)
-    weight_terms(acts[pl.ds(6 + 24 * core, 28), :W, :], first, 0)
+    weight_terms(narrowed(hidden[144:816], 24, -4), second[192:768], 24, 1)
+    image_band = acts[pl.ds(6 + 24 * core, 28), :W, :].reshape(28 * W, 256)
+    weight_terms(narrowed(image_band, W, -6), first[8:32].reshape(24 * 16, 256), 16, 0)
     send[...] = terms[1 - core].reshape(2, 8, 288, 128)
     keep[...] = terms[core].reshape(2, 8, 288, 128)
 
@@ -258,7 +237,7 @@
             outs[8 * half + 4 - 4 * at[4] + k, 288:, :] = image_got[half, k]
 
 
-def regroup_kernel(at, *rest):
+def regroup_kernel(*rest):
     pieces, windows, columns = rest
     total = None
     for j in range(16):
@@ -287,7 +266,7 @@
         windows[z, 80:, :] = rest[16 * z : 16 * z + 16].astype(BF16)
 
 
-def finish_kernel(scale, at, pieces, image_out, grad_one, grad_two, wide):
+def finish_kernel(scale, pieces, image_out, grad_one, grad_two, wide):
     total = None
     for z in range(8):
         parts = [pieces[z, k : k + 16, :].astype(F32) for k in (48, 64, 80)]
@@ -340,7 +319,7 @@
         + [pltpu.VMEM((144, 16), BF16)] * 2
         + [pltpu.SemaphoreType.DMA((4,))],
         [rows_first(image), rows_first(cotangent), *filters],
-        at,
+        room=63,
         space=pltpu.HBM,
     )
     pieces = call(
@@ -348,7 +327,6 @@
         shape((16, 432, 128)),
         [pltpu.VMEM((384, 128), F32), pltpu.VMEM((48, 128), F32)],
         [exchanged(pieces, "z")],
-        at,
     )
     pieces = exchanged(pieces, TORUS)
     send, keep, image_send, image_keep = call(
@@ -357,10 +335,10 @@
         [
             pltpu.VMEM((64, 48, 256), BF16),
             pltpu.VMEM((18, 16, 16, 256), BF16),
-            pltpu.VMEM((40, W, 256), F32),
-            pltpu.VMEM((40, W, 256), BF16),
-            pltpu.VMEM((40, W, 256), BF16),
-            pltpu.VMEM((40, W, 256), BF16),
+            pltpu.VMEM((40, 16, 256), F32),
+            pltpu.VMEM((40 * 24, 256), BF16),
+            pltpu.VMEM((40 * 24, 256), BF16),
+            pltpu.VMEM((40, 16, 256), BF16),
             pltpu.VMEM((3, 40, 16, 256), BF16),
             pltpu.VMEM((2, 2, 8, 18, 16, 128), BF16),
             pltpu.VMEM((24, 16, 256), BF16),
@@ -381,14 +359,12 @@
         shape((8, 96, 128)),
         [pltpu.VMEM((256, 128), F32)],
         [exchanged(pieces, TORUS)],
-        at,
     )
     image_grad, *filter_grads = call(
         functools.partial(finish_kernel, scale),
         [shape((48, 1280)), shape((144, 16), F32), shape((144, 16), F32)],
         [pltpu.VMEM((48, 1536), F32)],
         [exchanged(pieces, "z")],
-        at,
     )
     grad_one, grad_two = (
         jnp.transpose(g.reshape(9, 16, 16), (1, 0, 2)) for g in filter_grads

time: 117 us -> 111 us (0.949)
  local copies, waits for them, and re-layouts: 3.42 us -> 0.08 us
  Pallas kernels: 16.7 us -> 13.5 us
    unnamed x8 -> x0, local copies, waits for them, and re-layouts: 3.34 us -> none
    pallas_call x6, Pallas kernels: 16.7 us -> 13.5 us  [call(): pl.pallas_call(kernel, out_shape=outs, in_specs=where, out_specs=jax.tree...]
where the time goes in v3:
time: 111 us; the launch traced here: 110 us
  blocking collectives  88.9 us (80%)
  Pallas kernels  13.5 us (12%)
  waiting for transfers between devices  6.08 us (5%)
    all_to_all x4, blocking collectives, exchanged(): return lax.all_to_all(array, axes, split_axis=0, concat_axis=0, tiled=True)  88.9 us
    pallas_call x6, Pallas kernels, call(): pl.pallas_call(kernel, out_shape=outs, in_specs=where, out_specs=jax.tree...  13.5 us
    ppermute x3, waiting for transfers between devices, swapped(): return lax.ppermute(array, 'core', [(0, 1), (1, 0)])  6.08 us
  transfers between devices with their start and end apart: 3, of which 2 were waited for; matrix products, arithmetic and copies ran while one was open for 0% of the time, Pallas kernels for 0%

profile of v3, /device:TPU:8, one launch (start us, length us, event | category | flops | bytes accessed | tf_op | source)
XLA Modules:
  0.0 109.8 jit_solution(10366458727654313070)
XLA Ops:
  0.6 2.0 %shard_map.67 = bf16[8,64,384]{2,1,0:T(8,128)(2,1)} custom-call(bf16[48,1280]{1,0:T(8,128)(2,1)} %bitcast.26, bf16[48,1280]{1,0:T(8,128)(2,1)} %bitcast.27, bf16[144,16]{1,0:T(8,128)(2,1)} %bitcast.28, bf16[144,16]{1,0:T(8,128)(2,1)} %bitcast.29), custom_call_target="tpu_custom_call" | custom-call | tf_op jit(solution)/shard_map/pallas_call | solution.py:27
  2.6 23.2 %all_to_all.20.rest_0_ = bf16[8,64,384]{2,1,0:T(8,128)(2,1)S(1)} all-to-all(bf16[8,64,384]{2,1,0:T(8,128)(2,1)} %shard_map.67), channel_id=1, replica_groups=mesh['yh'=2,'z'=8,'yl'=2,'x'=4,'core'=2] {'z'}, dimensions={0} | all-to-all | bytes 786432 | tf_op jit(solution)/shard_map/all_to_all | solution.py:298
  25.8 0.5 shard_map.68
  26.2 29.5 %all_to_all.21.rest_0_ = bf16[16,432,128]{2,1,0:T(8,128)(2,1)S(1)} all-to-all(bf16[16,432,128]{2,1,0:T(8,128)(2,1)S(1)} %shard_map.68), channel_id=1, replica_groups=mesh['yh'=2,'z'=8,'yl'=2,'x'=4,'core'=2] {'yh','yl','x'}, dimensions={0} | all-to-all | bytes 3538944 | tf_op jit(solution)/shard_map/all_to_all | solution.py:298
  55.7 0.0 collective-permute-start
  55.7 0.1 stack.23.at
  55.8 3.6 %collective-permute-done.rest_1_ = bf16[16,432,128]{2,1,0:T(8,128)(2,1)S(1)} collective-permute-done((bf16[16,432,128]{2,1,0:T(8,128)(2,1)S(1)}, bf16[16,432,128]{2,1,0:T(8,128)(2,1)S(1)}, u32[]{:S(2)}, u32[]{:S(2)}) %collective-permute-start) | collective-permute-done | bytes 1769504 | tf_op jit(solution)/shard_map/ppermute | solution.py:302
  59.4 8.7 %shard_map.69 = (bf16[2,8,288,128]{3,2,1,0:T(8,128)(2,1)S(1)}, bf16[2,8,288,128]{3,2,1,0:T(8,128)(2,1)S(1)}, bf16[2,4,48,128]{3,2,1,0:T(8,128)(2,1)S(1)}, bf16[2,4,48,128]{3,2,1,0:T(8,128)(2,1)S(1)}) custom-call(s32[5]{0:T(128)S(1)} %stack.23.at, bf16[16,432,128]{2,1,0:T(8,128)(2,1)S(1)} %all_to_all.21.rest_0_, ...), custom_call_target="tpu_custom_call" | custom-call | tf_op jit(solution)/shard_map/pallas_call | solution.py:27
  68.0 0.2 collective-permute-start.1
  68.2 0.4 collective-permute-start.2
  68.6 2.5 %collective-permute-done.2.image_got = bf16[2,4,48,128]{3,2,1,0:T(8,128)(2,1)S(1)} collective-permute-done((bf16[2,4,48,128]{3,2,1,0:T(8,128)(2,1)S(1)}, bf16[2,4,48,128]{3,2,1,0:T(8,128)(2,1)S(1)}, u32[]{:S(2)}, u32[]{:S(2)}) %collective-permute-start.2) | collective-permute-done | bytes 98336 | tf_op jit(solution)/shard_map/ppermute | solution.py:302
  71.1 0.0 collective-permute-done.1.got
  71.1 0.8 shard_map.70
  72.0 24.1 %all_to_all.22.rest_0_ = bf16[16,336,128]{2,1,0:T(8,128)(2,1)S(1)} all-to-all(bf16[16,336,128]{2,1,0:T(8,128)(2,1)S(1)} %shard_map.70), channel_id=1, replica_groups=mesh['yh'=2,'z'=8,'yl'=2,'x'=4,'core'=2] {'yh','yl','x'}, dimensions={0} | all-to-all | bytes 2752512 | tf_op jit(solution)/shard_map/all_to_all | solution.py:298
  96.0 0.5 shard_map.71
  96.6 12.2 %all_to_all.23.pieces = bf16[8,96,128]{2,1,0:T(8,128)(2,1)S(1)} all-to-all(bf16[8,96,128]{2,1,0:T(8,128)(2,1)S(1)} %shard_map.71), channel_id=1, replica_groups=mesh['yh'=2,'z'=8,'yl'=2,'x'=4,'core'=2] {'z'}, dimensions={0} | all-to-all | bytes 393216 | tf_op jit(solution)/shard_map/all_to_all | solution.py:298
  108.8 1.0 shard_map.72
Async XLA Ops:
  55.7 3.7 %collective-permute-start = (bf16[16,432,128]{2,1,0:T(8,128)(2,1)S(1)}, bf16[16,432,128]{2,1,0:T(8,128)(2,1)S(1)}, u32[]{:S(2)}, u32[]{:S(2)}) collective-permute-start(bf16[16,432,128]{2,1,0:T(8,128)(2,1)S(1)} %all_to_all.21.rest_0_), channel_id=1, source_target_pairs={{0,1},{1,0},{2,3},{3,2},{4,5},{5,4},{6,7},{7,6},{8,9},{9,8},{10,11... | collective-permute-start | bytes 5308424 | tf_op jit(solution)/shard_map/ppermute | solution.py:302
  68.0 3.1 %collective-permute-start.1 = (bf16[2,8,288,128]{3,2,1,0:T(8,128)(2,1)S(1)}, bf16[2,8,288,128]{3,2,1,0:T(8,128)(2,1)S(1)}, u32[]{:S(2)}, u32[]{:S(2)}) collective-permute-start(bf16[2,8,288,128]{3,2,1,0:T(8,128)(2,1)S(1)} %get-tuple-element.11), channel_id=1, source_target_pairs={{0,1},{1,0},{2,3},{3,2},{4,5},{5,4},{6,7},{7,6},{8,9},{9,8},{10,11... | collective-permute-start | bytes 3538952 | tf_op jit(solution)/shard_map/ppermute | solution.py:302
  68.2 2.9 %collective-permute-start.2 = (bf16[2,4,48,128]{3,2,1,0:T(8,128)(2,1)S(1)}, bf16[2,4,48,128]{3,2,1,0:T(8,128)(2,1)S(1)}, u32[]{:S(2)}, u32[]{:S(2)}) collective-permute-start(bf16[2,4,48,128]{3,2,1,0:T(8,128)(2,1)S(1)} %get-tuple-element.13), channel_id=1, source_target_pairs={{0,1},{1,0},{2,3},{3,2},{4,5},{5,4},{6,7},{7,6},{8,9},{9,8},{10,11... | collective-permute-start | bytes 294920 | tf_op jit(solution)/shard_map/ppermute | solution.py:302

commit v4 on v3

--- a/solution.py
+++ b/solution.py
@@ -19,15 +19,11 @@
 W = 32
 
 
-def call(kernel, outs, scratch, args, prefetch=None, room=10, space=pltpu.VMEM):
-    where = [pl.BlockSpec(memory_space=space)] * len(args)
-    if prefetch is not None:
-        where = [pl.BlockSpec(memory_space=pltpu.SMEM)] + where
-        args = [prefetch, *args]
+def call(kernel, outs, scratch, args, room=10, space=pltpu.VMEM):
     return pl.pallas_call(
         kernel,
         out_shape=outs,
-        in_specs=where,
+        in_specs=[pl.BlockSpec(memory_space=space)] * len(args),
         out_specs=jax.tree.map(lambda _: pl.BlockSpec(memory_space=pltpu.VMEM), outs),
         scratch_shapes=scratch,
         compiler_params=pltpu.CompilerParams(vmem_limit_bytes=room * 2**20),
@@ -64,7 +60,9 @@
         ]
         + [jnp.zeros((16, 96), F32)],
         axis=1,
-    ).astype(BF16)
+    )
+    ends = pltpu.roll(pieces[:, 256:], 88, 1)
+    ends = jnp.concatenate([ends, ends, ends], axis=0)
     for wide, source in ((image_wide, image), (cotangent_wide, cotangent)):
         wide[:, :256] = jnp.zeros((48, 256), F32)
         wide[:, 1536:] = jnp.zeros((48, 256), F32)
@@ -77,19 +75,26 @@
         second = 256 + 160 * z - 4 - 176
         base = second // 128 * 128
         right = pltpu.roll(cotangent_wide[:, base : base + 512], 512 - (second - base), 1)[:, :384]
-        windows[z, :48, :] = jnp.where(lane < 176, left, right).astype(BF16)
-        windows[z, 48:, :] = pieces
+        both = jnp.where(lane < 176, left, right)
+        windows[z, :48, :] = both[:, :128].astype(BF16)
+        windows[z, 48:96, :] = both[:, 128:256].astype(BF16)
+        windows[z, 96:144, :] = jnp.where(lane[:, :128] < 88, both[:, 256:], ends).astype(BF16)
+        windows[z, 144:160, :] = pieces[:, :128].astype(BF16)
+        windows[z, 160:, :] = pieces[:, 128:256].astype(BF16)
 
 
 def turn_kernel(*rest):
     held, outs, turned, chunk = rest
     for i in range(3):
-        turned[...] = held[:, 16 * i : 16 * i + 16, :].reshape(128, 384).astype(F32).T
+        parts = [held[:, k + 16 * i : k + 16 * i + 16, :].reshape(128, 128) for k in (0, 48, 96)]
+        turned[...] = jnp.concatenate(parts, axis=1).astype(F32).T
         for j in range(16):
             chunk[:32, :] = turned[10 * j : 10 * j + 32, :]
             chunk[26:48, :] = turned[176 + 10 * j : 198 + 10 * j, :]
             outs[j, 48 * i : 48 * i + 48, :] = chunk[...].astype(BF16)
-    filters = held[:, 48:, :].reshape(128, 384).astype(F32).T[:288].astype(BF16)
+    parts = [held[:, k : k + 16, :].reshape(128, 128).astype(F32) for k in (144, 160, 96)]
+    parts[2] = pltpu.roll(parts[2], 40, 1)
+    filters = jnp.concatenate(parts, axis=1).T[:288].astype(BF16)
     for j in range(16):
         outs[j, 144:, :] = filters
 
@@ -120,11 +125,12 @@
     return s * (1.0 + v * (1.0 - s))
 
 
-def conv_kernel(at, *rest):
+def conv_kernel(*rest):
     own, other = rest[:2]
     send, keep, image_send, image_keep = rest[2:6]
-    acts, wides, pre, hidden, second, first, mine, terms, image_rows = rest[6:]
-    z, y, x, core = (at[k] for k in range(1, 5))
+    acts, wides, pre, hidden, second, first, mine, terms, image_rows, packed = rest[6:]
+    yh, z, yl, x, core = (lax.axis_index(a) for a in AXES)
+    y = 2 * yh + yl
     acts[:8] = jnp.zeros((8, 48, 256), BF16)
     acts[56:] = jnp.zeros((8, 48, 256), BF16)
     for pieces, side in ((own, core), (other, 1 - core)):
@@ -163,17 +169,12 @@
         value = value * sigmoid(value) * mask_24
         hidden[flat(start, rows)] = value.reshape(rows * 24, 256).astype(BF16)
 
-    def second_step(k, _):
-        rows = 14
-        start = 8 - 4 * core + rows * k
-        band = jnp.concatenate([hidden[flat(start + 2 * i - 2, rows)] for i in range(3)], axis=-1)
-        value = tapped(band, wide_two, (2, 0, -2), False).reshape(rows, 24, 256)
-        got = acts[pl.ds(start + 24 * core, rows), 16:, :].astype(F32)[:, 8:, :]
-        value = got * silu_slope(value) * mask_24
-        second[flat(start, rows)] = value.reshape(rows * 24, 256).astype(BF16)
-        return 0
-
-    lax.fori_loop(0, 2, second_step, 0)
+    start = 8 - 4 * core
+    band = jnp.concatenate([hidden[flat(start + 2 * i - 2, 28)] for i in range(3)], axis=-1)
+    value = tapped(band, wide_two, (2, 0, -2), False).reshape(28, 24, 256)
+    got = acts[pl.ds(start + 24 * core, 28), 16:, :].astype(F32)[:, 8:, :]
+    value = got * silu_slope(value) * mask_24
+    second[flat(start, 28)] = value.reshape(28 * 24, 256).astype(BF16)
 
     start = 8 - 2 * core
     band = jnp.concatenate([second[flat(start - 2 * i + 2, 26)] for i in range(3)], axis=-1)
@@ -183,13 +184,14 @@
 
     band = jnp.concatenate([first[10 - 2 * i : 34 - 2 * i] for i in range(3)], axis=-1)
     value = tapped(band.reshape(384, 768), wide_one, (-4, -2, 0), True)
-    image_rows[...] = value.reshape(24, 16, 256).astype(BF16)
+    image_rows[...] = value.reshape(24, 16, 256)
     for side, out in ((1 - core, image_send), (core, image_keep)):
         for k in range(4):
             for half in range(2):
-                out[half, k] = image_rows[
-                    pl.ds(6 * k + 3 * side, 3), :, 128 * half : 128 * half + 128
-                ].reshape(48, 128)
+                lines = image_rows[pl.ds(6 * k + 3 * side, 3), :, 128 * half : 128 * half + 128]
+                for i in range(3):
+                    packed[10 * i : 10 * i + 16, :] = lines[i]
+                out[half, k] = packed[:32, :].astype(BF16)
 
     def narrowed(values, columns, shift):
         rows = values.shape[0] // columns
@@ -227,18 +229,20 @@
     keep[...] = terms[core].reshape(2, 8, 288, 128)
 
 
-def scatter_kernel(at, keep, got, image_keep, image_got, outs):
+def scatter_kernel(keep, got, image_keep, image_got, outs):
+    core = lax.axis_index("core")
     for j in range(16):
         half, q = j // 8, j % 8
         outs[j, :288, :] = (keep[half, q].astype(F32) + got[half, q].astype(F32)).astype(BF16)
     for half in range(2):
         for k in range(4):
-            outs[8 * half + 4 * at[4] + k, 288:, :] = image_keep[half, k]
-            outs[8 * half + 4 - 4 * at[4] + k, 288:, :] = image_got[half, k]
+            outs[8 * half + 4 * core + k, 288:, :] = image_keep[half, k]
+            outs[8 * half + 4 - 4 * core + k, 288:, :] = image_got[half, k]
 
 
 def regroup_kernel(*rest):
-    pieces, windows, columns = rest
+    pieces, windows, columns, unpacked = rest
+    unpacked[...] = pieces[:, 288:, :].astype(F32)
     total = None
     for j in range(16):
         term = pieces[j, :288, :].astype(F32)
@@ -252,9 +256,7 @@
     columns[...] = jnp.zeros((256, 128), F32)
     for i in range(3):
         for j in range(16):
-            columns[10 * j : 10 * j + 16, :] = pieces[j, 288 + 16 * i : 304 + 16 * i, :].astype(
-                F32
-            )
+            columns[10 * j : 10 * j + 10, :] = unpacked[j, 10 * i : 10 * i + 10, :]
         turned = columns[...].T
         for z in range(8):
             windows[z, 16 * i : 16 * i + 16, :] = turned[16 * z : 16 * z + 16, :128].astype(BF16)
@@ -304,16 +306,13 @@
 
 def local(image, filter_one, filter_two, cotangent):
     scale = 1.0 / math.sqrt(48 * 1280)
-    yh, z, yl, x, core = (lax.axis_index(a) for a in AXES)
-    at = jnp.stack([yh, z, 2 * yh + yl, x, core]).astype(jnp.int32)
-
     def rows_first(a):
         return jnp.transpose(a, (1, 0, 2)).reshape(48, 1280)
 
     filters = [jnp.transpose(f, (1, 0, 2)).reshape(144, 16) for f in (filter_one, filter_two)]
     pieces = call(
         windows_kernel,
-        shape((8, 64, 384)),
+        shape((8, 176, 128)),
         [pltpu.VMEM((48, 1792), F32)] * 2
         + [pltpu.VMEM((48, 1280), BF16)] * 2
         + [pltpu.VMEM((144, 16), BF16)] * 2
@@ -331,7 +330,7 @@
     pieces = exchanged(pieces, TORUS)
     send, keep, image_send, image_keep = call(
         conv_kernel,
-        [shape((2, 8, 288, 128))] * 2 + [shape((2, 4, 48, 128))] * 2,
+        [shape((2, 8, 288, 128))] * 2 + [shape((2, 4, 32, 128))] * 2,
         [
             pltpu.VMEM((64, 48, 256), BF16),
             pltpu.VMEM((18, 16, 16, 256), BF16),
@@ -341,23 +340,22 @@
             pltpu.VMEM((40, 16, 256), BF16),
             pltpu.VMEM((3, 40, 16, 256), BF16),
             pltpu.VMEM((2, 2, 8, 18, 16, 128), BF16),
-            pltpu.VMEM((24, 16, 256), BF16),
+            pltpu.VMEM((24, 16, 256), F32),
+            pltpu.VMEM((40, 128), F32),
         ],
         [pieces, swapped(pieces)],
-        at,
-        28,
+        room=28,
     )
     pieces = call(
         scatter_kernel,
-        shape((16, 336, 128)),
+        shape((16, 320, 128)),
         [],
         [keep, swapped(send), image_keep, swapped(image_send)],
-        at,
     )
     pieces = call(
         regroup_kernel,
         shape((8, 96, 128)),
-        [pltpu.VMEM((256, 128), F32)],
+        [pltpu.VMEM((256, 128), F32), pltpu.VMEM((16, 32, 128), F32)],
         [exchanged(pieces, TORUS)],
     )
     image_grad, *filter_grads = call(

time: 111 us -> 108 us (0.973)
  blocking collectives: 88.9 us -> 87.4 us
  Pallas kernels: 13.5 us -> 12.2 us
    all_to_all x4, blocking collectives: 88.9 us -> 87.4 us  [exchanged(): return lax.all_to_all(array, axes, split_axis=0, concat_axis=0, tiled=True)]
    pallas_call x6, Pallas kernels: 13.5 us -> 12.2 us  [call(): pl.pallas_call(kernel, out_shape=outs, in_specs=[pl.BlockSpec(memory_spac...]
where the time goes in v4:
time: 108 us; the launch traced here: 107 us
  blocking collectives  87.4 us (81%)
  Pallas kernels  12.2 us (11%)
  waiting for transfers between devices  6.12 us (6%)
    all_to_all x4, blocking collectives, exchanged(): return lax.all_to_all(array, axes, split_axis=0, concat_axis=0, tiled=True)  87.4 us
    pallas_call x6, Pallas kernels, call(): pl.pallas_call(kernel, out_shape=outs, in_specs=[pl.BlockSpec(memory_spac...  12.2 us
    ppermute x3, waiting for transfers between devices, swapped(): return lax.ppermute(array, 'core', [(0, 1), (1, 0)])  6.12 us
  transfers between devices with their start and end apart: 3, of which 2 were waited for; matrix products, arithmetic and copies ran while one was open for 0% of the time, Pallas kernels for 0%

profile of v4, /device:TPU:8, one launch (start us, length us, event | category | flops | bytes accessed | tf_op | source)
XLA Modules:
  0.0 107.0 jit_solution(16284778705918039989)
XLA Ops:
  0.6 2.1 %shard_map.67 = bf16[8,176,128]{2,1,0:T(8,128)(2,1)} custom-call(bf16[48,1280]{1,0:T(8,128)(2,1)} %bitcast.21, bf16[48,1280]{1,0:T(8,128)(2,1)} %bitcast.22, bf16[144,16]{1,0:T(8,128)(2,1)} %bitcast.23, bf16[144,16]{1,0:T(8,128)(2,1)} %bitcast.24), custom_call_target="tpu_custom_call" | custom-call | tf_op jit(solution)/shard_map/pallas_call | solution.py:23
  2.7 22.5 %all_to_all.20.rest_0_ = bf16[8,176,128]{2,1,0:T(8,128)(2,1)S(1)} all-to-all(bf16[8,176,128]{2,1,0:T(8,128)(2,1)} %shard_map.67), channel_id=1, replica_groups=mesh['yh'=2,'z'=8,'yl'=2,'x'=4,'core'=2] {'z'}, dimensions={0} | all-to-all | bytes 720896 | tf_op jit(solution)/shard_map/all_to_all | solution.py:300
  25.1 0.5 shard_map.68
  25.6 29.4 %all_to_all.21.rest_0_ = bf16[16,432,128]{2,1,0:T(8,128)(2,1)S(1)} all-to-all(bf16[16,432,128]{2,1,0:T(8,128)(2,1)S(1)} %shard_map.68), channel_id=1, replica_groups=mesh['yh'=2,'z'=8,'yl'=2,'x'=4,'core'=2] {'yh','yl','x'}, dimensions={0} | all-to-all | bytes 3538944 | tf_op jit(solution)/shard_map/all_to_all | solution.py:300
  55.0 0.0 collective-permute-start
  55.0 3.7 %collective-permute-done.rest_1_ = bf16[16,432,128]{2,1,0:T(8,128)(2,1)S(1)} collective-permute-done((bf16[16,432,128]{2,1,0:T(8,128)(2,1)S(1)}, bf16[16,432,128]{2,1,0:T(8,128)(2,1)S(1)}, u32[]{:S(2)}, u32[]{:S(2)}) %collective-permute-start) | collective-permute-done | bytes 1769504 | tf_op jit(solution)/shard_map/ppermute | solution.py:304
  58.7 7.9 %shard_map.69 = (bf16[2,8,288,128]{3,2,1,0:T(8,128)(2,1)S(1)}, bf16[2,8,288,128]{3,2,1,0:T(8,128)(2,1)S(1)}, bf16[2,4,32,128]{3,2,1,0:T(8,128)(2,1)S(1)}, bf16[2,4,32,128]{3,2,1,0:T(8,128)(2,1)S(1)}) custom-call(bf16[16,432,128]{2,1,0:T(8,128)(2,1)S(1)} %all_to_all.21.rest_0_, bf16[16,432,128]{2,1,0:T(8,128)(2,1)S(1)} %collective-permute-done.rest_1_), custom_call_target="tpu_custom_call" | custom-call | tf_op jit(solution)/shard_map/pallas_call | solution.py:23
  66.5 0.4 collective-permute-start.1
  66.9 0.2 collective-permute-start.2
  67.1 2.4 %collective-permute-done.2.image_got = bf16[2,4,32,128]{3,2,1,0:T(8,128)(2,1)S(1)} collective-permute-done((bf16[2,4,32,128]{3,2,1,0:T(8,128)(2,1)S(1)}, bf16[2,4,32,128]{3,2,1,0:T(8,128)(2,1)S(1)}, u32[]{:S(2)}, u32[]{:S(2)}) %collective-permute-start.2) | collective-permute-done | bytes 65568 | tf_op jit(solution)/shard_map/ppermute | solution.py:304
  69.6 0.0 collective-permute-done.1.got
  69.6 0.3 shard_map.70
  69.9 23.4 %all_to_all.22.rest_0_ = bf16[16,320,128]{2,1,0:T(8,128)(2,1)S(1)} all-to-all(bf16[16,320,128]{2,1,0:T(8,128)(2,1)S(1)} %shard_map.70), channel_id=1, replica_groups=mesh['yh'=2,'z'=8,'yl'=2,'x'=4,'core'=2] {'yh','yl','x'}, dimensions={0} | all-to-all | bytes 2621440 | tf_op jit(solution)/shard_map/all_to_all | solution.py:300
  93.2 0.6 shard_map.71
  93.8 12.2 %all_to_all.23.pieces = bf16[8,96,128]{2,1,0:T(8,128)(2,1)S(1)} all-to-all(bf16[8,96,128]{2,1,0:T(8,128)(2,1)S(1)} %shard_map.71), channel_id=1, replica_groups=mesh['yh'=2,'z'=8,'yl'=2,'x'=4,'core'=2] {'z'}, dimensions={0} | all-to-all | bytes 393216 | tf_op jit(solution)/shard_map/all_to_all | solution.py:300
  106.0 1.0 shard_map.72
Async XLA Ops:
  55.0 3.7 %collective-permute-start = (bf16[16,432,128]{2,1,0:T(8,128)(2,1)S(1)}, bf16[16,432,128]{2,1,0:T(8,128)(2,1)S(1)}, u32[]{:S(2)}, u32[]{:S(2)}) collective-permute-start(bf16[16,432,128]{2,1,0:T(8,128)(2,1)S(1)} %all_to_all.21.rest_0_), channel_id=1, source_target_pairs={{0,1},{1,0},{2,3},{3,2},{4,5},{5,4},{6,7},{7,6},{8,9},{9,8},{10,11... | collective-permute-start | bytes 5308424 | tf_op jit(solution)/shard_map/ppermute | solution.py:304
  66.5 3.0 %collective-permute-start.1 = (bf16[2,8,288,128]{3,2,1,0:T(8,128)(2,1)S(1)}, bf16[2,8,288,128]{3,2,1,0:T(8,128)(2,1)S(1)}, u32[]{:S(2)}, u32[]{:S(2)}) collective-permute-start(bf16[2,8,288,128]{3,2,1,0:T(8,128)(2,1)S(1)} %get-tuple-element.11), channel_id=1, source_target_pairs={{0,1},{1,0},{2,3},{3,2},{4,5},{5,4},{6,7},{7,6},{8,9},{9,8},{10,11... | collective-permute-start | bytes 3538952 | tf_op jit(solution)/shard_map/ppermute | solution.py:304
  66.9 2.7 %collective-permute-start.2 = (bf16[2,4,32,128]{3,2,1,0:T(8,128)(2,1)S(1)}, bf16[2,4,32,128]{3,2,1,0:T(8,128)(2,1)S(1)}, u32[]{:S(2)}, u32[]{:S(2)}) collective-permute-start(bf16[2,4,32,128]{3,2,1,0:T(8,128)(2,1)S(1)} %get-tuple-element.13), channel_id=1, source_target_pairs={{0,1},{1,0},{2,3},{3,2},{4,5},{5,4},{6,7},{7,6},{8,9},{9,8},{10,11... | collective-permute-start | bytes 196616 | tf_op jit(solution)/shard_map/ppermute | solution.py:304

commit v5 on v4

--- a/solution.py
+++ b/solution.py
@@ -12,7 +12,12 @@
 AXES = ("yh", "z", "yl", "x", "core")
 CHAN = ("yh", "z")
 STRIP = ("yl", "x", "core")
-TORUS = ("yh", "yl", "x")
+RING = [(y, x if y % 2 == 0 else 3 - x) for y in range(4) for x in range(4)]
+TORUS = [
+    [(((y // 2 * 8 + z) * 2 + y % 2) * 4 + x) * 2 + core for y, x in RING]
+    for z in range(8)
+    for core in range(2)
+]
 F32 = jnp.float32
 BF16 = jnp.bfloat16
 
@@ -134,9 +139,9 @@
     acts[:8] = jnp.zeros((8, 48, 256), BF16)
     acts[56:] = jnp.zeros((8, 48, 256), BF16)
     for pieces, side in ((own, core), (other, 1 - core)):
-        for j in range(16):
-            half = j // 8
-            strip = 2 * (j % 8) + side
+        for j, (at_y, at_x) in enumerate(RING):
+            half = at_y // 2
+            strip = 2 * (4 * (at_y % 2) + at_x) + side
             lanes = slice(half * 128, half * 128 + 128)
             acts[pl.ds(3 * strip + 8, 3), :, lanes] = pieces[j, :144, :].reshape(3, 48, 128)
             wides[:, strip, :, lanes] = pieces[j, 144:, :].reshape(18, 16, 128)
@@ -146,7 +151,7 @@
     hidden[pl.ds(pl.multiple_of(24 * rows_out, 48), 192)] = jnp.zeros((192, 256), BF16)
     second[pl.ds(pl.multiple_of(24 * rows_out, 48), 192)] = jnp.zeros((192, 256), BF16)
     first[pl.ds(rows_out, 8)] = jnp.zeros((8, 16, 256), BF16)
-    left = 160 * z + 10 * (4 * y + x) - 8
+    left = 160 * z + 10 * (4 * y + jnp.where(yl == 0, x, 3 - x)) - 8
 
     def mask(begin, columns):
         c = lax.broadcasted_iota(jnp.int32, (1, columns, 256), 1) + (left + begin)
@@ -231,13 +236,15 @@
 
 def scatter_kernel(keep, got, image_keep, image_got, outs):
     core = lax.axis_index("core")
-    for j in range(16):
-        half, q = j // 8, j % 8
+    for j, (y, x) in enumerate(RING):
+        half, q = y // 2, 4 * (y % 2) + x
         outs[j, :288, :] = (keep[half, q].astype(F32) + got[half, q].astype(F32)).astype(BF16)
     for half in range(2):
         for k in range(4):
-            outs[8 * half + 4 * core + k, 288:, :] = image_keep[half, k]
-            outs[8 * half + 4 - 4 * core + k, 288:, :] = image_got[half, k]
+            near = 8 * half + 4 * core + jnp.where(core == 0, k, 3 - k)
+            far = 8 * half + 4 - 4 * core + jnp.where(core == 1, k, 3 - k)
+            outs[near, 288:, :] = image_keep[half, k]
+            outs[far, 288:, :] = image_got[half, k]
 
 
 def regroup_kernel(*rest):
@@ -296,8 +303,10 @@
     image_out[...] = wide[:, :1280].astype(BF16)
 
 
-def exchanged(array, axes):
-    return lax.all_to_all(array, axes, split_axis=0, concat_axis=0, tiled=True)
+def exchanged(array, axes, groups=None):
+    return lax.all_to_all(
+        array, axes, split_axis=0, concat_axis=0, axis_index_groups=groups, tiled=True
+    )
 
 
 def swapped(array):
@@ -317,8 +326,10 @@
         + [pltpu.VMEM((48, 1280), BF16)] * 2
         + [pltpu.VMEM((144, 16), BF16)] * 2
         + [pltpu.SemaphoreType.DMA((4,))],
-        [rows_first(image), rows_first(cotangent), *filters],
-        room=63,
+        [
+            pltpu.with_memory_space_constraint(a, pltpu.HBM)
+            for a in (rows_first(image), rows_first(cotangent), *filters)
+        ],
         space=pltpu.HBM,
     )
     pieces = call(
@@ -327,7 +338,7 @@
         [pltpu.VMEM((384, 128), F32), pltpu.VMEM((48, 128), F32)],
         [exchanged(pieces, "z")],
     )
-    pieces = exchanged(pieces, TORUS)
+    pieces = exchanged(pieces, AXES, TORUS)
     send, keep, image_send, image_keep = call(
         conv_kernel,
         [shape((2, 8, 288, 128))] * 2 + [shape((2, 4, 32, 128))] * 2,
@@ -356,7 +367,7 @@
         regroup_kernel,
         shape((8, 96, 128)),
         [pltpu.VMEM((256, 128), F32), pltpu.VMEM((16, 32, 128), F32)],
-        [exchanged(pieces, TORUS)],
+        [exchanged(pieces, AXES, TORUS)],
     )
     image_grad, *filter_grads = call(
         functools.partial(finish_kernel, scale),

time: 108 us -> 106 us (0.981)
  no operation moved by 1% of the time
where the time goes in v5:
time: 106 us
  blocking collectives  87.2 us (82%)
  Pallas kernels  11.4 us (11%)
  waiting for transfers between devices  6.12 us (6%)
    all_to_all x4, blocking collectives, exchanged(): lax.all_to_all(array, axes, split_axis=0, concat_axis=0, axis_index_group...  87.2 us
    pallas_call x6, Pallas kernels, call(): pl.pallas_call(kernel, out_shape=outs, in_specs=[pl.BlockSpec(memory_spac...  11.4 us
    ppermute x3, waiting for transfers between devices, swapped(): return lax.ppermute(array, 'core', [(0, 1), (1, 0)])  6.12 us
  transfers between devices with their start and end apart: 3, of which 2 were waited for; matrix products, arithmetic and copies ran while one was open for 0% of the time, Pallas kernels for 0%

profile of v5, /device:TPU:8, one launch (start us, length us, event | category | flops | bytes accessed | tf_op | source)
XLA Modules:
  0.0 105.9 jit_solution(3177886863040486498)
XLA Ops:
  0.6 1.3 %shard_map.67 = bf16[8,176,128]{2,1,0:T(8,128)(2,1)S(1)} custom-call(bf16[48,1280]{1,0:T(8,128)(2,1)} %bitcast.21, bf16[48,1280]{1,0:T(8,128)(2,1)} %bitcast.22, bf16[144,16]{1,0:T(8,128)(2,1)} %bitcast.23, bf16[144,16]{1,0:T(8,128)(2,1)} %bitcast.24), custom_call_target="tpu_custom_call" | custom-call | tf_op jit(solution)/shard_map/pallas_call | solution.py:28
  1.9 22.2 %all_to_all.20.rest_0_ = bf16[8,176,128]{2,1,0:T(8,128)(2,1)S(1)} all-to-all(bf16[8,176,128]{2,1,0:T(8,128)(2,1)S(1)} %shard_map.67), channel_id=1, replica_groups=mesh['yh'=2,'z'=8,'yl'=2,'x'=4,'core'=2] {'z'}, dimensions={0} | all-to-all | bytes 720896 | tf_op jit(solution)/shard_map/all_to_all | solution.py:307
  24.2 0.5 shard_map.68
  24.7 29.1 %all_to_all.21.rest_0_ = bf16[16,432,128]{2,1,0:T(8,128)(2,1)S(1)} all-to-all(bf16[16,432,128]{2,1,0:T(8,128)(2,1)S(1)} %shard_map.68), channel_id=1, replica_groups={{0,2,4,6,14,12,10,8,128,130,132,134,142,140,138,136},{1,3,5,7,15,13,11,..., dimensions={0} | all-to-all | bytes 3538944 | tf_op jit(solution)/shard_map/all_to_all | solution.py:307
  53.8 0.0 collective-permute-start
  53.8 3.7 %collective-permute-done.rest_1_ = bf16[16,432,128]{2,1,0:T(8,128)(2,1)S(1)} collective-permute-done((bf16[16,432,128]{2,1,0:T(8,128)(2,1)S(1)}, bf16[16,432,128]{2,1,0:T(8,128)(2,1)S(1)}, u32[]{:S(2)}, u32[]{:S(2)}) %collective-permute-start) | collective-permute-done | bytes 1769504 | tf_op jit(solution)/shard_map/ppermute | solution.py:313
  57.5 7.8 %shard_map.69 = (bf16[2,8,288,128]{3,2,1,0:T(8,128)(2,1)S(1)}, bf16[2,8,288,128]{3,2,1,0:T(8,128)(2,1)S(1)}, bf16[2,4,32,128]{3,2,1,0:T(8,128)(2,1)S(1)}, bf16[2,4,32,128]{3,2,1,0:T(8,128)(2,1)S(1)}) custom-call(bf16[16,432,128]{2,1,0:T(8,128)(2,1)S(1)} %all_to_all.21.rest_0_, bf16[16,432,128]{2,1,0:T(8,128)(2,1)S(1)} %collective-permute-done.rest_1_), custom_call_target="tpu_custom_call" | custom-call | tf_op jit(solution)/shard_map/pallas_call | solution.py:28
  65.3 0.3 collective-permute-start.1
  65.6 0.3 collective-permute-start.2
  65.9 2.4 %collective-permute-done.2.image_got = bf16[2,4,32,128]{3,2,1,0:T(8,128)(2,1)S(1)} collective-permute-done((bf16[2,4,32,128]{3,2,1,0:T(8,128)(2,1)S(1)}, bf16[2,4,32,128]{3,2,1,0:T(8,128)(2,1)S(1)}, u32[]{:S(2)}, u32[]{:S(2)}) %collective-permute-start.2) | collective-permute-done | bytes 65568 | tf_op jit(solution)/shard_map/ppermute | solution.py:313
  68.3 0.0 collective-permute-done.1.got
  68.3 0.3 shard_map.70
  68.6 23.4 %all_to_all.22.rest_0_ = bf16[16,320,128]{2,1,0:T(8,128)(2,1)S(1)} all-to-all(bf16[16,320,128]{2,1,0:T(8,128)(2,1)S(1)} %shard_map.70), channel_id=1, replica_groups={{0,2,4,6,14,12,10,8,128,130,132,134,142,140,138,136},{1,3,5,7,15,13,11,..., dimensions={0} | all-to-all | bytes 2621440 | tf_op jit(solution)/shard_map/all_to_all | solution.py:307
  92.0 0.6 shard_map.71
  92.5 12.4 %all_to_all.23.pieces = bf16[8,96,128]{2,1,0:T(8,128)(2,1)S(1)} all-to-all(bf16[8,96,128]{2,1,0:T(8,128)(2,1)S(1)} %shard_map.71), channel_id=1, replica_groups=mesh['yh'=2,'z'=8,'yl'=2,'x'=4,'core'=2] {'z'}, dimensions={0} | all-to-all | bytes 393216 | tf_op jit(solution)/shard_map/all_to_all | solution.py:307
  104.9 1.0 shard_map.72
Async XLA Ops:
  53.8 3.7 %collective-permute-start = (bf16[16,432,128]{2,1,0:T(8,128)(2,1)S(1)}, bf16[16,432,128]{2,1,0:T(8,128)(2,1)S(1)}, u32[]{:S(2)}, u32[]{:S(2)}) collective-permute-start(bf16[16,432,128]{2,1,0:T(8,128)(2,1)S(1)} %all_to_all.21.rest_0_), channel_id=1, source_target_pairs={{0,1},{1,0},{2,3},{3,2},{4,5},{5,4},{6,7},{7,6},{8,9},{9,8},{10,11... | collective-permute-start | bytes 5308424 | tf_op jit(solution)/shard_map/ppermute | solution.py:313
  65.3 3.0 %collective-permute-start.1 = (bf16[2,8,288,128]{3,2,1,0:T(8,128)(2,1)S(1)}, bf16[2,8,288,128]{3,2,1,0:T(8,128)(2,1)S(1)}, u32[]{:S(2)}, u32[]{:S(2)}) collective-permute-start(bf16[2,8,288,128]{3,2,1,0:T(8,128)(2,1)S(1)} %get-tuple-element.11), channel_id=1, source_target_pairs={{0,1},{1,0},{2,3},{3,2},{4,5},{5,4},{6,7},{7,6},{8,9},{9,8},{10,11... | collective-permute-start | bytes 3538952 | tf_op jit(solution)/shard_map/ppermute | solution.py:313
  65.6 2.7 %collective-permute-start.2 = (bf16[2,4,32,128]{3,2,1,0:T(8,128)(2,1)S(1)}, bf16[2,4,32,128]{3,2,1,0:T(8,128)(2,1)S(1)}, u32[]{:S(2)}, u32[]{:S(2)}) collective-permute-start(bf16[2,4,32,128]{3,2,1,0:T(8,128)(2,1)S(1)} %get-tuple-element.13), channel_id=1, source_target_pairs={{0,1},{1,0},{2,3},{3,2},{4,5},{5,4},{6,7},{7,6},{8,9},{9,8},{10,11... | collective-permute-start | bytes 196616 | tf_op jit(solution)/shard_map/ppermute | solution.py:313

commit v6 on v5

--- a/solution.py
+++ b/solution.py
@@ -133,11 +133,11 @@
 def conv_kernel(*rest):
     own, other = rest[:2]
     send, keep, image_send, image_keep = rest[2:6]
-    acts, wides, pre, hidden, second, first, mine, terms, image_rows, packed = rest[6:]
+    acts, wides, pre, hidden, second, first, mine, image_rows, packed = rest[6:]
     yh, z, yl, x, core = (lax.axis_index(a) for a in AXES)
     y = 2 * yh + yl
-    acts[:8] = jnp.zeros((8, 48, 256), BF16)
-    acts[56:] = jnp.zeros((8, 48, 256), BF16)
+    acts[6:8] = jnp.zeros((2, 48, 256), BF16)
+    acts[56:58] = jnp.zeros((2, 48, 256), BF16)
     for pieces, side in ((own, core), (other, 1 - core)):
         for j, (at_y, at_x) in enumerate(RING):
             half = at_y // 2
@@ -147,10 +147,10 @@
             wides[:, strip, :, lanes] = pieces[j, 144:, :].reshape(18, 16, 128)
     wide_one, wide_two = wides.at[:9], wides.at[9:]
 
-    rows_out = 32 * core
-    hidden[pl.ds(pl.multiple_of(24 * rows_out, 48), 192)] = jnp.zeros((192, 256), BF16)
-    second[pl.ds(pl.multiple_of(24 * rows_out, 48), 192)] = jnp.zeros((192, 256), BF16)
-    first[pl.ds(rows_out, 8)] = jnp.zeros((8, 16, 256), BF16)
+    rows_out = 6 + 26 * core
+    hidden[pl.ds(pl.multiple_of(24 * rows_out, 48), 48)] = jnp.zeros((48, 256), BF16)
+    second[pl.ds(pl.multiple_of(24 * rows_out, 48), 48)] = jnp.zeros((48, 256), BF16)
+    first[pl.ds(rows_out, 2)] = jnp.zeros((2, 16, 256), BF16)
     left = 160 * z + 10 * (4 * y + jnp.where(yl == 0, x, 3 - x)) - 8
 
     def mask(begin, columns):
@@ -162,8 +162,8 @@
 
     mask_24, mask_16 = mask(2, 24), mask(6, 16)
 
-    for k in range(2):
-        rows = (16, 14)[k]
+    for k in range(1):
+        rows = 30
         start = 8 - 6 * core + 16 * k
         band = jnp.concatenate(
             [acts[pl.ds(start + 24 * core + 2 * i - 2, rows), :W, :] for i in range(3)], axis=-1
@@ -213,13 +213,14 @@
         def step(i, _):
             for j in range(3):
                 rows = mine[j, pl.ds(8 - 2 * i, 28)].reshape(28 * 16, 256)
-                got = jnp.dot(turned, rows, preferred_element_type=F32).astype(BF16)
+                got = jnp.dot(turned, rows, preferred_element_type=F32)
                 got = got.reshape(8, 2, 16, 256)
-                for side in range(2):
-                    for half in range(2):
-                        terms[side, half, :, 9 * which + 3 * i + j] = got[
-                            :, side, :, 128 * half : 128 * half + 128
-                        ]
+                sent = jnp.where(core == 0, got[:, 1], got[:, 0])
+                kept = jnp.where(core == 0, got[:, 0], got[:, 1])
+                for half in range(2):
+                    lanes = slice(128 * half, 128 * half + 128)
+                    send[half, :, 9 * which + 3 * i + j] = sent[:, :, lanes].astype(BF16)
+                    keep[half, :, 9 * which + 3 * i + j] = kept[:, :, lanes].astype(BF16)
             return 0
 
         lax.fori_loop(0, 3, step, 0)
@@ -230,15 +231,14 @@
     weight_terms(narrowed(hidden[144:816], 24, -4), second[192:768], 24, 1)
     image_band = acts[pl.ds(6 + 24 * core, 28), :W, :].reshape(28 * W, 256)
     weight_terms(narrowed(image_band, W, -6), first[8:32].reshape(24 * 16, 256), 16, 0)
-    send[...] = terms[1 - core].reshape(2, 8, 288, 128)
-    keep[...] = terms[core].reshape(2, 8, 288, 128)
 
 
 def scatter_kernel(keep, got, image_keep, image_got, outs):
     core = lax.axis_index("core")
     for j, (y, x) in enumerate(RING):
         half, q = y // 2, 4 * (y % 2) + x
-        outs[j, :288, :] = (keep[half, q].astype(F32) + got[half, q].astype(F32)).astype(BF16)
+        total = keep[half, q].astype(F32) + got[half, q].astype(F32)
+        outs[j, :288, :] = total.reshape(288, 128).astype(BF16)
     for half in range(2):
         for k in range(4):
             near = 8 * half + 4 * core + jnp.where(core == 0, k, 3 - k)
@@ -341,7 +341,7 @@
     pieces = exchanged(pieces, AXES, TORUS)
     send, keep, image_send, image_keep = call(
         conv_kernel,
-        [shape((2, 8, 288, 128))] * 2 + [shape((2, 4, 32, 128))] * 2,
+        [shape((2, 8, 18, 16, 128))] * 2 + [shape((2, 4, 32, 128))] * 2,
         [
             pltpu.VMEM((64, 48, 256), BF16),
             pltpu.VMEM((18, 16, 16, 256), BF16),
@@ -350,7 +350,6 @@
             pltpu.VMEM((40 * 24, 256), BF16),
             pltpu.VMEM((40, 16, 256), BF16),
             pltpu.VMEM((3, 40, 16, 256), BF16),
-            pltpu.VMEM((2, 2, 8, 18, 16, 128), BF16),
             pltpu.VMEM((24, 16, 256), F32),
             pltpu.VMEM((40, 128), F32),
         ],

time: 106 us -> 106 us (level)
  no operation moved by 1% of the time
where the time goes in v6:
time: 106 us
  blocking collectives  87.2 us (82%)
  Pallas kernels  11.5 us (11%)
  waiting for transfers between devices  6.12 us (6%)
    all_to_all x4, blocking collectives, exchanged(): lax.all_to_all(array, axes, split_axis=0, concat_axis=0, axis_index_group...  87.2 us
    pallas_call x6, Pallas kernels, call(): pl.pallas_call(kernel, out_shape=outs, in_specs=[pl.BlockSpec(memory_spac...  11.5 us
    ppermute x3, waiting for transfers between devices, swapped(): return lax.ppermute(array, 'core', [(0, 1), (1, 0)])  6.12 us
  transfers between devices with their start and end apart: 3, of which 2 were waited for; matrix products, arithmetic and copies ran while one was open for 0% of the time, Pallas kernels for 0%

profile of v6, /device:TPU:8, one launch (start us, length us, event | category | flops | bytes accessed | tf_op | source)
XLA Modules:
  0.0 106.0 jit_solution(13032893776221654550)
XLA Ops:
  0.6 1.3 %shard_map.67 = bf16[8,176,128]{2,1,0:T(8,128)(2,1)S(1)} custom-call(bf16[48,1280]{1,0:T(8,128)(2,1)} %bitcast.21, bf16[48,1280]{1,0:T(8,128)(2,1)} %bitcast.22, bf16[144,16]{1,0:T(8,128)(2,1)} %bitcast.23, bf16[144,16]{1,0:T(8,128)(2,1)} %bitcast.24), custom_call_target="tpu_custom_call" | custom-call | tf_op jit(solution)/shard_map/pallas_call | solution.py:28
  1.9 22.2 %all_to_all.20.rest_0_ = bf16[8,176,128]{2,1,0:T(8,128)(2,1)S(1)} all-to-all(bf16[8,176,128]{2,1,0:T(8,128)(2,1)S(1)} %shard_map.67), channel_id=1, replica_groups=mesh['yh'=2,'z'=8,'yl'=2,'x'=4,'core'=2] {'z'}, dimensions={0} | all-to-all | bytes 720896 | tf_op jit(solution)/shard_map/all_to_all | solution.py:307
  24.2 0.5 shard_map.68
  24.7 29.1 %all_to_all.21.rest_0_ = bf16[16,432,128]{2,1,0:T(8,128)(2,1)S(1)} all-to-all(bf16[16,432,128]{2,1,0:T(8,128)(2,1)S(1)} %shard_map.68), channel_id=1, replica_groups={{0,2,4,6,14,12,10,8,128,130,132,134,142,140,138,136},{1,3,5,7,15,13,11,..., dimensions={0} | all-to-all | bytes 3538944 | tf_op jit(solution)/shard_map/all_to_all | solution.py:307
  53.8 0.0 collective-permute-start
  53.8 3.7 %collective-permute-done.rest_1_ = bf16[16,432,128]{2,1,0:T(8,128)(2,1)S(1)} collective-permute-done((bf16[16,432,128]{2,1,0:T(8,128)(2,1)S(1)}, bf16[16,432,128]{2,1,0:T(8,128)(2,1)S(1)}, u32[]{:S(2)}, u32[]{:S(2)}) %collective-permute-start) | collective-permute-done | bytes 1769504 | tf_op jit(solution)/shard_map/ppermute | solution.py:313
  57.5 7.9 %shard_map.69 = (bf16[2,8,18,16,128]{4,3,2,1,0:T(8,128)(2,1)S(1)}, bf16[2,8,18,16,128]{4,3,2,1,0:T(8,128)(2,1)S(1)}, bf16[2,4,32,128]{3,2,1,0:T(8,128)(2,1)S(1)}, bf16[2,4,32,128]{3,2,1,0:T(8,128)(2,1)S(1)}) custom-call(bf16[16,432,128]{2,1,0:T(8,128)(2,1)S(1)} %all_to_all.21.rest_0_, bf16[16,432,128]{2,1,0:T(8,128)(2,1)S(1)} %collective-permute-done.rest_1_), custom_call_target="tpu_custom_call" | custom-call | tf_op jit(solution)/shard_map/pallas_call | solution.py:28
  65.3 0.3 collective-permute-start.1
  65.7 0.3 collective-permute-start.2
  65.9 2.4 %collective-permute-done.2.image_got = bf16[2,4,32,128]{3,2,1,0:T(8,128)(2,1)S(1)} collective-permute-done((bf16[2,4,32,128]{3,2,1,0:T(8,128)(2,1)S(1)}, bf16[2,4,32,128]{3,2,1,0:T(8,128)(2,1)S(1)}, u32[]{:S(2)}, u32[]{:S(2)}) %collective-permute-start.2) | collective-permute-done | bytes 65568 | tf_op jit(solution)/shard_map/ppermute | solution.py:313
  68.4 0.0 collective-permute-done.1.got
  68.4 0.3 shard_map.70
  68.7 23.4 %all_to_all.22.rest_0_ = bf16[16,320,128]{2,1,0:T(8,128)(2,1)S(1)} all-to-all(bf16[16,320,128]{2,1,0:T(8,128)(2,1)S(1)} %shard_map.70), channel_id=1, replica_groups={{0,2,4,6,14,12,10,8,128,130,132,134,142,140,138,136},{1,3,5,7,15,13,11,..., dimensions={0} | all-to-all | bytes 2621440 | tf_op jit(solution)/shard_map/all_to_all | solution.py:307
  92.0 0.6 shard_map.71
  92.6 12.4 %all_to_all.23.pieces = bf16[8,96,128]{2,1,0:T(8,128)(2,1)S(1)} all-to-all(bf16[8,96,128]{2,1,0:T(8,128)(2,1)S(1)} %shard_map.71), channel_id=1, replica_groups=mesh['yh'=2,'z'=8,'yl'=2,'x'=4,'core'=2] {'z'}, dimensions={0} | all-to-all | bytes 393216 | tf_op jit(solution)/shard_map/all_to_all | solution.py:307
  105.0 1.0 shard_map.72
Async XLA Ops:
  53.8 3.7 %collective-permute-start = (bf16[16,432,128]{2,1,0:T(8,128)(2,1)S(1)}, bf16[16,432,128]{2,1,0:T(8,128)(2,1)S(1)}, u32[]{:S(2)}, u32[]{:S(2)}) collective-permute-start(bf16[16,432,128]{2,1,0:T(8,128)(2,1)S(1)} %all_to_all.21.rest_0_), channel_id=1, source_target_pairs={{0,1},{1,0},{2,3},{3,2},{4,5},{5,4},{6,7},{7,6},{8,9},{9,8},{10,11... | collective-permute-start | bytes 5308424 | tf_op jit(solution)/shard_map/ppermute | solution.py:313
  65.3 3.0 %collective-permute-start.1 = (bf16[2,8,18,16,128]{4,3,2,1,0:T(8,128)(2,1)S(1)}, bf16[2,8,18,16,128]{4,3,2,1,0:T(8,128)(2,1)S(1)}, u32[]{:S(2)}, u32[]{:S(2)}) collective-permute-start(bf16[2,8,18,16,128]{4,3,2,1,0:T(8,128)(2,1)S(1)} %get-tuple-element.11), channel_id=1, source_target_pairs={{0,1},{1,0},{2,3},{3,2},{4,5},{5,4},{6,7},{7,6},{8,9},{9,8},{10,11... | collective-permute-start | bytes 3538952 | tf_op jit(solution)/shard_map/ppermute | solution.py:313
  65.7 2.7 %collective-permute-start.2 = (bf16[2,4,32,128]{3,2,1,0:T(8,128)(2,1)S(1)}, bf16[2,4,32,128]{3,2,1,0:T(8,128)(2,1)S(1)}, u32[]{:S(2)}, u32[]{:S(2)}) collective-permute-start(bf16[2,4,32,128]{3,2,1,0:T(8,128)(2,1)S(1)} %get-tuple-element.13), channel_id=1, source_target_pairs={{0,1},{1,0},{2,3},{3,2},{4,5},{5,4},{6,7},{7,6},{8,9},{9,8},{10,11... | collective-permute-start | bytes 196616 | tf_op jit(solution)/shard_map/ppermute | solution.py:313

commit v7 on v6

--- a/solution.py
+++ b/solution.py
@@ -132,8 +132,8 @@
 
 def conv_kernel(*rest):
     own, other = rest[:2]
-    send, keep, image_send, image_keep = rest[2:6]
-    acts, wides, pre, hidden, second, first, mine, image_rows, packed = rest[6:]
+    send, keep = rest[2:4]
+    acts, wides, pre, hidden, second, first, mine, image_rows, packed = rest[4:]
     yh, z, yl, x, core = (lax.axis_index(a) for a in AXES)
     y = 2 * yh + yl
     acts[6:8] = jnp.zeros((2, 48, 256), BF16)
@@ -190,13 +190,15 @@
     band = jnp.concatenate([first[10 - 2 * i : 34 - 2 * i] for i in range(3)], axis=-1)
     value = tapped(band.reshape(384, 768), wide_one, (-4, -2, 0), True)
     image_rows[...] = value.reshape(24, 16, 256)
-    for side, out in ((1 - core, image_send), (core, image_keep)):
+    for side, out in ((1 - core, send), (core, keep)):
         for k in range(4):
             for half in range(2):
                 lines = image_rows[pl.ds(6 * k + 3 * side, 3), :, 128 * half : 128 * half + 128]
                 for i in range(3):
                     packed[10 * i : 10 * i + 16, :] = lines[i]
-                out[half, k] = packed[:32, :].astype(BF16)
+                out[half, 144 + 2 * k : 146 + 2 * k] = (
+                    packed[:32, :].astype(BF16).reshape(2, 16, 128)
+                )
 
     def narrowed(values, columns, shift):
         rows = values.shape[0] // columns
@@ -219,8 +221,10 @@
                 kept = jnp.where(core == 0, got[:, 0], got[:, 1])
                 for half in range(2):
                     lanes = slice(128 * half, 128 * half + 128)
-                    send[half, :, 9 * which + 3 * i + j] = sent[:, :, lanes].astype(BF16)
-                    keep[half, :, 9 * which + 3 * i + j] = kept[:, :, lanes].astype(BF16)
+                    for q in range(8):
+                        place = 18 * q + 9 * which + 3 * i + j
+                        send[half, place] = sent[q, :, lanes].astype(BF16)
+                        keep[half, place] = kept[q, :, lanes].astype(BF16)
             return 0
 
         lax.fori_loop(0, 3, step, 0)
@@ -233,18 +237,20 @@
     weight_terms(narrowed(image_band, W, -6), first[8:32].reshape(24 * 16, 256), 16, 0)
 
 
-def scatter_kernel(keep, got, image_keep, image_got, outs):
+def scatter_kernel(keep, got, outs):
     core = lax.axis_index("core")
     for j, (y, x) in enumerate(RING):
         half, q = y // 2, 4 * (y % 2) + x
-        total = keep[half, q].astype(F32) + got[half, q].astype(F32)
+        part = slice(18 * q, 18 * q + 18)
+        total = keep[half, part].astype(F32) + got[half, part].astype(F32)
         outs[j, :288, :] = total.reshape(288, 128).astype(BF16)
     for half in range(2):
         for k in range(4):
             near = 8 * half + 4 * core + jnp.where(core == 0, k, 3 - k)
             far = 8 * half + 4 - 4 * core + jnp.where(core == 1, k, 3 - k)
-            outs[near, 288:, :] = image_keep[half, k]
-            outs[far, 288:, :] = image_got[half, k]
+            part = slice(144 + 2 * k, 146 + 2 * k)
+            outs[near, 288:, :] = keep[half, part].reshape(32, 128)
+            outs[far, 288:, :] = got[half, part].reshape(32, 128)
 
 
 def regroup_kernel(*rest):
@@ -339,9 +345,9 @@
         [exchanged(pieces, "z")],
     )
     pieces = exchanged(pieces, AXES, TORUS)
-    send, keep, image_send, image_keep = call(
+    send, keep = call(
         conv_kernel,
-        [shape((2, 8, 18, 16, 128))] * 2 + [shape((2, 4, 32, 128))] * 2,
+        [shape((2, 152, 16, 128))] * 2,
         [
             pltpu.VMEM((64, 48, 256), BF16),
             pltpu.VMEM((18, 16, 16, 256), BF16),
@@ -360,7 +366,7 @@
         scatter_kernel,
         shape((16, 320, 128)),
         [],
-        [keep, swapped(send), image_keep, swapped(image_send)],
+        [keep, swapped(send)],
     )
     pieces = call(
         regroup_kernel,

time: 106 us -> 106 us (level)
    ppermute x3 -> x2, waiting for transfers between devices: 6.12 us -> 6.37 us  [swapped(): return lax.ppermute(array, 'core', [(0, 1), (1, 0)])]
  transfers between devices with their start and end apart: 3 -> 2, of which waited for: 2 -> 2; matrix products, arithmetic and copies ran while one was open for 0% -> 0% of each run, Pallas kernels for 0% -> 0%
where the time goes in v7:
time: 106 us
  blocking collectives  87.2 us (82%)
  Pallas kernels  11.5 us (11%)
  waiting for transfers between devices  6.37 us (6%)
    all_to_all x4, blocking collectives, exchanged(): lax.all_to_all(array, axes, split_axis=0, concat_axis=0, axis_index_group...  87.2 us
    pallas_call x6, Pallas kernels, call(): pl.pallas_call(kernel, out_shape=outs, in_specs=[pl.BlockSpec(memory_spac...  11.5 us
    ppermute x2, waiting for transfers between devices, swapped(): return lax.ppermute(array, 'core', [(0, 1), (1, 0)])  6.37 us
  transfers between devices with their start and end apart: 2, of which 2 were waited for; matrix products, arithmetic and copies ran while one was open for 0% of the time, Pallas kernels for 0%

profile of v7, /device:TPU:8, one launch (start us, length us, event | category | flops | bytes accessed | tf_op | source)
XLA Modules:
  0.0 106.0 jit_solution(17726025466981800159)
XLA Ops:
  0.6 1.3 %shard_map.67 = bf16[8,176,128]{2,1,0:T(8,128)(2,1)S(1)} custom-call(bf16[48,1280]{1,0:T(8,128)(2,1)} %bitcast.21, bf16[48,1280]{1,0:T(8,128)(2,1)} %bitcast.22, bf16[144,16]{1,0:T(8,128)(2,1)} %bitcast.23, bf16[144,16]{1,0:T(8,128)(2,1)} %bitcast.24), custom_call_target="tpu_custom_call" | custom-call | tf_op jit(solution)/shard_map/pallas_call | solution.py:28
  1.9 22.2 %all_to_all.20.rest_0_ = bf16[8,176,128]{2,1,0:T(8,128)(2,1)S(1)} all-to-all(bf16[8,176,128]{2,1,0:T(8,128)(2,1)S(1)} %shard_map.67), channel_id=1, replica_groups=mesh['yh'=2,'z'=8,'yl'=2,'x'=4,'core'=2] {'z'}, dimensions={0} | all-to-all | bytes 720896 | tf_op jit(solution)/shard_map/all_to_all | solution.py:313
  24.2 0.5 shard_map.68
  24.7 29.1 %all_to_all.21.rest_0_ = bf16[16,432,128]{2,1,0:T(8,128)(2,1)S(1)} all-to-all(bf16[16,432,128]{2,1,0:T(8,128)(2,1)S(1)} %shard_map.68), channel_id=1, replica_groups={{0,2,4,6,14,12,10,8,128,130,132,134,142,140,138,136},{1,3,5,7,15,13,11,..., dimensions={0} | all-to-all | bytes 3538944 | tf_op jit(solution)/shard_map/all_to_all | solution.py:313
  53.8 0.0 collective-permute-start
  53.8 3.7 %collective-permute-done.rest_1_ = bf16[16,432,128]{2,1,0:T(8,128)(2,1)S(1)} collective-permute-done((bf16[16,432,128]{2,1,0:T(8,128)(2,1)S(1)}, bf16[16,432,128]{2,1,0:T(8,128)(2,1)S(1)}, u32[]{:S(2)}, u32[]{:S(2)}) %collective-permute-start) | collective-permute-done | bytes 1769504 | tf_op jit(solution)/shard_map/ppermute | solution.py:319
  57.5 7.9 %shard_map.69 = (bf16[2,152,16,128]{3,2,1,0:T(8,128)(2,1)S(1)}, bf16[2,152,16,128]{3,2,1,0:T(8,128)(2,1)S(1)}) custom-call(bf16[16,432,128]{2,1,0:T(8,128)(2,1)S(1)} %all_to_all.21.rest_0_, bf16[16,432,128]{2,1,0:T(8,128)(2,1)S(1)} %collective-permute-done.rest_1_), custom_call_target="tpu_custom_call" | custom-call | tf_op jit(solution)/shard_map/pallas_call | solution.py:28
  65.3 0.3 collective-permute-start.1
  65.7 2.7 %collective-permute-done.1.got = bf16[2,152,16,128]{3,2,1,0:T(8,128)(2,1)S(1)} collective-permute-done((bf16[2,152,16,128]{3,2,1,0:T(8,128)(2,1)S(1)}, bf16[2,152,16,128]{3,2,1,0:T(8,128)(2,1)S(1)}, u32[]{:S(2)}, u32[]{:S(2)}) %collective-permute-start.1) | collective-permute-done | bytes 1245216 | tf_op jit(solution)/shard_map/ppermute | solution.py:319
  68.4 0.3 shard_map.70
  68.6 23.4 %all_to_all.22.rest_0_ = bf16[16,320,128]{2,1,0:T(8,128)(2,1)S(1)} all-to-all(bf16[16,320,128]{2,1,0:T(8,128)(2,1)S(1)} %shard_map.70), channel_id=1, replica_groups={{0,2,4,6,14,12,10,8,128,130,132,134,142,140,138,136},{1,3,5,7,15,13,11,..., dimensions={0} | all-to-all | bytes 2621440 | tf_op jit(solution)/shard_map/all_to_all | solution.py:313
  92.0 0.6 shard_map.71
  92.6 12.4 %all_to_all.23.pieces = bf16[8,96,128]{2,1,0:T(8,128)(2,1)S(1)} all-to-all(bf16[8,96,128]{2,1,0:T(8,128)(2,1)S(1)} %shard_map.71), channel_id=1, replica_groups=mesh['yh'=2,'z'=8,'yl'=2,'x'=4,'core'=2] {'z'}, dimensions={0} | all-to-all | bytes 393216 | tf_op jit(solution)/shard_map/all_to_all | solution.py:313
  105.0 1.0 shard_map.72
Async XLA Ops:
  53.8 3.7 %collective-permute-start = (bf16[16,432,128]{2,1,0:T(8,128)(2,1)S(1)}, bf16[16,432,128]{2,1,0:T(8,128)(2,1)S(1)}, u32[]{:S(2)}, u32[]{:S(2)}) collective-permute-start(bf16[16,432,128]{2,1,0:T(8,128)(2,1)S(1)} %all_to_all.21.rest_0_), channel_id=1, source_target_pairs={{0,1},{1,0},{2,3},{3,2},{4,5},{5,4},{6,7},{7,6},{8,9},{9,8},{10,11... | collective-permute-start | bytes 5308424 | tf_op jit(solution)/shard_map/ppermute | solution.py:319
  65.3 3.0 %collective-permute-start.1 = (bf16[2,152,16,128]{3,2,1,0:T(8,128)(2,1)S(1)}, bf16[2,152,16,128]{3,2,1,0:T(8,128)(2,1)S(1)}, u32[]{:S(2)}, u32[]{:S(2)}) collective-permute-start(bf16[2,152,16,128]{3,2,1,0:T(8,128)(2,1)S(1)} %get-tuple-element.9), channel_id=1, source_target_pairs={{0,1},{1,0},{2,3},{3,2},{4,5},{5,4},{6,7},{7,6},{8,9},{9,8},{10,11... | collective-permute-start | bytes 3735560 | tf_op jit(solution)/shard_map/ppermute | solution.py:319

commit v8 on v6

--- a/solution.py
+++ b/solution.py
@@ -211,10 +211,10 @@
             mine[j, 8:32] = jnp.where(kept, shifted, 0.0).astype(BF16)
 
         def step(i, _):
+            rows = [mine[j, pl.ds(8 - 2 * i, 28)].reshape(28 * 16, 256) for j in range(3)]
+            every = jnp.dot(turned, jnp.concatenate(rows, axis=1), preferred_element_type=F32)
             for j in range(3):
-                rows = mine[j, pl.ds(8 - 2 * i, 28)].reshape(28 * 16, 256)
-                got = jnp.dot(turned, rows, preferred_element_type=F32)
-                got = got.reshape(8, 2, 16, 256)
+                got = every[:, 256 * j : 256 * j + 256].reshape(8, 2, 16, 256)
                 sent = jnp.where(core == 0, got[:, 1], got[:, 0])
                 kept = jnp.where(core == 0, got[:, 0], got[:, 1])
                 for half in range(2):

time: 106 us -> 106 us (level)
  no operation moved by 1% of the time
where the time goes in v8:
time: 106 us
  blocking collectives  87.2 us (82%)
  Pallas kernels  11.5 us (11%)
  waiting for transfers between devices  6.12 us (6%)
    all_to_all x4, blocking collectives, exchanged(): lax.all_to_all(array, axes, split_axis=0, concat_axis=0, axis_index_group...  87.2 us
    pallas_call x6, Pallas kernels, call(): pl.pallas_call(kernel, out_shape=outs, in_specs=[pl.BlockSpec(memory_spac...  11.5 us
    ppermute x3, waiting for transfers between devices, swapped(): return lax.ppermute(array, 'core', [(0, 1), (1, 0)])  6.12 us
  transfers between devices with their start and end apart: 3, of which 2 were waited for; matrix products, arithmetic and copies ran while one was open for 0% of the time, Pallas kernels for 0%

profile of v8, /device:TPU:8, one launch (start us, length us, event | category | flops | bytes accessed | tf_op | source)
XLA Modules:
  0.0 106.0 jit_solution(13032893776221654550)
XLA Ops:
  0.6 1.3 %shard_map.67 = bf16[8,176,128]{2,1,0:T(8,128)(2,1)S(1)} custom-call(bf16[48,1280]{1,0:T(8,128)(2,1)} %bitcast.21, bf16[48,1280]{1,0:T(8,128)(2,1)} %bitcast.22, bf16[144,16]{1,0:T(8,128)(2,1)} %bitcast.23, bf16[144,16]{1,0:T(8,128)(2,1)} %bitcast.24), custom_call_target="tpu_custom_call" | custom-call | tf_op jit(solution)/shard_map/pallas_call | solution.py:28
  1.9 22.2 %all_to_all.20.rest_0_ = bf16[8,176,128]{2,1,0:T(8,128)(2,1)S(1)} all-to-all(bf16[8,176,128]{2,1,0:T(8,128)(2,1)S(1)} %shard_map.67), channel_id=1, replica_groups=mesh['yh'=2,'z'=8,'yl'=2,'x'=4,'core'=2] {'z'}, dimensions={0} | all-to-all | bytes 720896 | tf_op jit(solution)/shard_map/all_to_all | solution.py:307
  24.2 0.5 shard_map.68
  24.7 29.1 %all_to_all.21.rest_0_ = bf16[16,432,128]{2,1,0:T(8,128)(2,1)S(1)} all-to-all(bf16[16,432,128]{2,1,0:T(8,128)(2,1)S(1)} %shard_map.68), channel_id=1, replica_groups={{0,2,4,6,14,12,10,8,128,130,132,134,142,140,138,136},{1,3,5,7,15,13,11,..., dimensions={0} | all-to-all | bytes 3538944 | tf_op jit(solution)/shard_map/all_to_all | solution.py:307
  53.8 0.0 collective-permute-start
  53.8 3.7 %collective-permute-done.rest_1_ = bf16[16,432,128]{2,1,0:T(8,128)(2,1)S(1)} collective-permute-done((bf16[16,432,128]{2,1,0:T(8,128)(2,1)S(1)}, bf16[16,432,128]{2,1,0:T(8,128)(2,1)S(1)}, u32[]{:S(2)}, u32[]{:S(2)}) %collective-permute-start) | collective-permute-done | bytes 1769504 | tf_op jit(solution)/shard_map/ppermute | solution.py:313
  57.5 7.9 %shard_map.69 = (bf16[2,8,18,16,128]{4,3,2,1,0:T(8,128)(2,1)S(1)}, bf16[2,8,18,16,128]{4,3,2,1,0:T(8,128)(2,1)S(1)}, bf16[2,4,32,128]{3,2,1,0:T(8,128)(2,1)S(1)}, bf16[2,4,32,128]{3,2,1,0:T(8,128)(2,1)S(1)}) custom-call(bf16[16,432,128]{2,1,0:T(8,128)(2,1)S(1)} %all_to_all.21.rest_0_, bf16[16,432,128]{2,1,0:T(8,128)(2,1)S(1)} %collective-permute-done.rest_1_), custom_call_target="tpu_custom_call" | custom-call | tf_op jit(solution)/shard_map/pallas_call | solution.py:28
  65.3 0.3 collective-permute-start.1
  65.7 0.3 collective-permute-start.2
  65.9 2.4 %collective-permute-done.2.image_got = bf16[2,4,32,128]{3,2,1,0:T(8,128)(2,1)S(1)} collective-permute-done((bf16[2,4,32,128]{3,2,1,0:T(8,128)(2,1)S(1)}, bf16[2,4,32,128]{3,2,1,0:T(8,128)(2,1)S(1)}, u32[]{:S(2)}, u32[]{:S(2)}) %collective-permute-start.2) | collective-permute-done | bytes 65568 | tf_op jit(solution)/shard_map/ppermute | solution.py:313
  68.4 0.0 collective-permute-done.1.got
  68.4 0.3 shard_map.70
  68.7 23.4 %all_to_all.22.rest_0_ = bf16[16,320,128]{2,1,0:T(8,128)(2,1)S(1)} all-to-all(bf16[16,320,128]{2,1,0:T(8,128)(2,1)S(1)} %shard_map.70), channel_id=1, replica_groups={{0,2,4,6,14,12,10,8,128,130,132,134,142,140,138,136},{1,3,5,7,15,13,11,..., dimensions={0} | all-to-all | bytes 2621440 | tf_op jit(solution)/shard_map/all_to_all | solution.py:307
  92.0 0.6 shard_map.71
  92.6 12.4 %all_to_all.23.pieces = bf16[8,96,128]{2,1,0:T(8,128)(2,1)S(1)} all-to-all(bf16[8,96,128]{2,1,0:T(8,128)(2,1)S(1)} %shard_map.71), channel_id=1, replica_groups=mesh['yh'=2,'z'=8,'yl'=2,'x'=4,'core'=2] {'z'}, dimensions={0} | all-to-all | bytes 393216 | tf_op jit(solution)/shard_map/all_to_all | solution.py:307
  105.0 1.0 shard_map.72
Async XLA Ops:
  53.8 3.7 %collective-permute-start = (bf16[16,432,128]{2,1,0:T(8,128)(2,1)S(1)}, bf16[16,432,128]{2,1,0:T(8,128)(2,1)S(1)}, u32[]{:S(2)}, u32[]{:S(2)}) collective-permute-start(bf16[16,432,128]{2,1,0:T(8,128)(2,1)S(1)} %all_to_all.21.rest_0_), channel_id=1, source_target_pairs={{0,1},{1,0},{2,3},{3,2},{4,5},{5,4},{6,7},{7,6},{8,9},{9,8},{10,11... | collective-permute-start | bytes 5308424 | tf_op jit(solution)/shard_map/ppermute | solution.py:313
  65.3 3.0 %collective-permute-start.1 = (bf16[2,8,18,16,128]{4,3,2,1,0:T(8,128)(2,1)S(1)}, bf16[2,8,18,16,128]{4,3,2,1,0:T(8,128)(2,1)S(1)}, u32[]{:S(2)}, u32[]{:S(2)}) collective-permute-start(bf16[2,8,18,16,128]{4,3,2,1,0:T(8,128)(2,1)S(1)} %get-tuple-element.11), channel_id=1, source_target_pairs={{0,1},{1,0},{2,3},{3,2},{4,5},{5,4},{6,7},{7,6},{8,9},{9,8},{10,11... | collective-permute-start | bytes 3538952 | tf_op jit(solution)/shard_map/ppermute | solution.py:313
  65.7 2.7 %collective-permute-start.2 = (bf16[2,4,32,128]{3,2,1,0:T(8,128)(2,1)S(1)}, bf16[2,4,32,128]{3,2,1,0:T(8,128)(2,1)S(1)}, u32[]{:S(2)}, u32[]{:S(2)}) collective-permute-start(bf16[2,4,32,128]{3,2,1,0:T(8,128)(2,1)S(1)} %get-tuple-element.13), channel_id=1, source_target_pairs={{0,1},{1,0},{2,3},{3,2},{4,5},{5,4},{6,7},{7,6},{8,9},{9,8},{10,11... | collective-permute-start | bytes 196616 | tf_op jit(solution)/shard_map/ppermute | solution.py:313
